TPU v7x, 128 devices: a whole 4x4x4 slice. The times are simulated.
128 devices in a mesh: mod: 16 (over x, y_hi, core), sp: 8 (over y_lo, z).
Axes of the slice: x: 4, y: 4 (y_hi: 2, y_lo: 2; y = y_hi * 2 + y_lo), z: 4, core: 2. Of those that a mesh axis runs over, the one named last changes fastest.
Arguments:
- images: bfloat16 [16, 512, 64, 256], P('mod', None, 'sp'), may hold values from -6 to 6
- conv_first: bfloat16 [16, 256, 256], P('mod'), may hold values from -0.375 to 0.375
- conv_second: bfloat16 [16, 4096, 256], P('mod'), may hold values from -0.09375 to 0.09375
- project: bfloat16 [16, 256, 512], P('mod'), may hold values from -0.375 to 0.375
- whiten: bfloat16 [16, 512, 256], P('mod'), may hold values from -0.25 to 0.25
- valid_mask: int32 [16, 512, 16, 4], P('mod', None, 'sp'), may hold values 0 or 1
- scene_index: int32 [512], replicated, may hold values from 0 to 63
Outputs:
- target: float32 [512, 256], P('sp')
- grad_view: bfloat16 [16, 512, 256], P('mod', 'sp')
- grad_whiten: float32 [16, 512, 256], P('mod', 'sp')
Inputs may be any that keep to these rules, and one draw needn't show every extreme that they name: `valid_mask`: 1 where a pixel of the encoded map is cloud-free.
All inputs are finite; a program needn't handle non-finite values. No bound on the sum of `valid_mask` on one device may be relied on, other than what follows from the above.
Results may differ from a plain program's by a relative error of at most 0.028.
Values may be sent and summed in bfloat16 or wider, within the bound.
No kernel may reach another device: no remote copies, remote signals or barrier semaphores. Data moves between devices by JAX's collectives and lax.ppermute only.
A program may use at most 192 MiB of HBM per device.

v0:
```python
import jax
import jax.numpy as jnp
from jax import lax
from jax.sharding import PartitionSpec as P

BANDS = 16
CH = 256
SCENES = 64


def extended(x, sides, width):
    for axis, dim in sides:
        size, length = (lax.axis_size(axis), x.shape[dim])
        up = [(i, (i + 1) % size) for i in range(size - 1)]
        down = [(j, i) for i, j in up]
        last = lax.slice_in_dim(x, length - width, length, axis=dim)
        leading = lax.slice_in_dim(x, 0, width, axis=dim)
        before = lax.ppermute(last, axis, up)
        after = lax.ppermute(leading, axis, down)
        x = jnp.concatenate([before, x, after], axis=dim)
    return x


def stride_conv(padded, weight, depth, per_tap):
    count, rows_in, wide = padded.shape
    columns = wide // depth
    sided = jnp.pad(padded, ((0, 0), (0, 0), (depth, depth)))
    paired = sided.reshape(count, rows_in, columns // 2 + 1, 2 * depth)
    joined = jnp.concatenate([paired[:, :, :-1], paired[:, :, 1:]], axis=-1)
    rows_out = (rows_in - 2) // 2
    span = 4 * depth
    taps = [joined[:, offset : offset + 2 * rows_out : 2] for offset in range(4)]
    if per_tap:
        total = jnp.zeros((count * rows_out * (columns // 2), weight.shape[1]), jnp.float32)
        for offset in range(4):
            total = total + jnp.dot(
                taps[offset].reshape(-1, span),
                weight[offset * span : (offset + 1) * span],
                preferred_element_type=jnp.float32,
            )
    else:
        total = jnp.dot(
            jnp.concatenate(taps, axis=-1).reshape(-1, 4 * span),
            weight,
            preferred_element_type=jnp.float32,
        )
    return (
        jnp.maximum(total, 0.0)
        .astype(jnp.bfloat16)
        .reshape(count, rows_out, columns // 2 * weight.shape[1])
    )


def make_view(feat, onehot_rows, scene_sums, counts, whiten_w):
    means = scene_sums / jnp.maximum(counts, 1.0)[:, None]
    panel = (feat - jnp.dot(onehot_rows, means, precision=lax.Precision.HIGHEST)).astype(
        jnp.bfloat16
    )
    raw = jnp.dot(panel, whiten_w, preferred_element_type=jnp.float32)
    scale = 1.0 / jnp.sqrt(jnp.mean(raw * raw, axis=-1, keepdims=True) + 1e-05)
    return (panel, scale, (raw * scale).astype(jnp.bfloat16))


def on_device(images, conv_first, conv_second, project, whiten, valid_mask, scene_index):
    samples = images.shape[1]
    share = samples // lax.axis_size("sp")
    first_row = lax.axis_index("sp") * share
    padded = extended(images[0], (("sp", 1),), 1)
    first = stride_conv(padded, conv_first[0], BANDS, False)
    widened = extended(first, (("sp", 1),), 1)
    second = stride_conv(widened, conv_second[0], CH, True)
    pixels = second.reshape(samples, -1, CH)
    mask_rows = valid_mask[0].reshape(samples, -1).astype(jnp.bfloat16)
    cells = pixels.shape[1] * lax.axis_size("sp")
    pooled_part = (
        jnp.einsum("npc,np->nc", pixels, mask_rows, preferred_element_type=jnp.float32) / cells
    )
    pooled_rows = lax.psum_scatter(pooled_part, "sp", scatter_dimension=0, tiled=True)
    onehot = (scene_index[:, None] == jnp.arange(SCENES, dtype=jnp.int32)[None, :]).astype(
        jnp.float32
    )
    counts = jnp.sum(onehot, axis=0)
    project_w = project[0]
    whiten_w = whiten[0]
    feat = jnp.dot(pooled_rows.astype(jnp.bfloat16), project_w, preferred_element_type=jnp.float32)
    onehot_rows = lax.dynamic_slice_in_dim(onehot, first_row, share, 0)
    local_sums = jnp.dot(onehot_rows.T, feat, precision=lax.Precision.HIGHEST)
    scene_sums = lax.psum(local_sums, "sp")
    panel_rows, scale_rows, view_rows = make_view(feat, onehot_rows, scene_sums, counts, whiten_w)
    view = lax.all_gather(view_rows, "sp", axis=0, tiled=True)
    width = view.shape[1]
    eye = jnp.eye(width, dtype=jnp.float32)
    total = lax.psum(view.astype(jnp.float32).astype(jnp.bfloat16), "mod").astype(jnp.float32)
    piece = lax.all_gather(view[None], "mod", axis=0, tiled=True)
    blocks = jnp.einsum("nk,pnl->pkl", view, piece, preferred_element_type=jnp.float32) / samples
    piece_rows = lax.dynamic_slice_in_dim(piece, first_row, share, 1).astype(jnp.float32)
    coupling = jnp.einsum("pnl,pkl->nk", piece_rows, blocks - eye, precision=lax.Precision.HIGHEST)
    mean_view = total / lax.axis_size("mod")
    gram = jnp.dot(mean_view.T, mean_view, precision=lax.Precision.HIGHEST) / samples + 0.001 * eye
    lower = jnp.linalg.cholesky(gram)
    mean_rows = lax.dynamic_slice_in_dim(mean_view, first_row, share, 0)
    target_rows = jax.scipy.linalg.solve_triangular(lower, mean_rows.T, lower=True).T
    view_f = view_rows.astype(jnp.float32)
    grad_full = view_f - target_rows + coupling
    inner = jnp.mean(grad_full * view_f, axis=-1, keepdims=True)
    grad_raw = ((grad_full - view_f * inner) * scale_rows).astype(jnp.bfloat16)
    grad_w = lax.psum_scatter(
        jnp.dot(panel_rows.T, grad_raw, preferred_element_type=jnp.float32).astype(jnp.bfloat16),
        "sp",
        scatter_dimension=0,
        tiled=True,
    ).astype(jnp.float32)
    return (target_rows, grad_full.astype(jnp.bfloat16)[None], grad_w[None])


def solution(mesh):
    placed = (
        P("mod", None, "sp", None),
        P("mod", None, None),
        P("mod", None, None),
        P("mod", None, None),
        P("mod", None, None),
        P("mod", None, "sp", None),
        P(),
    )
    return jax.shard_map(
        on_device,
        mesh=mesh,
        in_specs=placed,
        out_specs=(P("sp", None), P("mod", "sp", None), P("mod", "sp", None)),
        check_vma=False,
    )
```

profile of v0, /device:TPU:0, one launch (start us, length us, event | category | flops | bytes accessed | tf_op | source)
XLA Modules:
  0.0 805.3 jit_solution(15705632569282844667)
XLA Ops:
  7.2 3.0 copy.29
  10.3 3.9 collective-permute-start
  14.3 1.3 collective-permute-start.1
  15.6 4.2 collective-permute-done
  19.8 4.3 collective-permute-done.1
  24.1 0.3 fusion.16
  24.4 0.6 fusion.75
  25.0 0.7 pad_maximum_fusion.2
  25.7 1.0 fusion.74
  26.7 3.6 pad_maximum_fusion.1
  30.3 14.7 %copy.30 = bf16[512,4,8,256]{3,2,1,0:T(8,128)(2,1)} copy(bf16[512,4,8,256]{0,3,2,1:T(8,128)(2,1)} %pad_maximum_fusion.1) | data formatting | bytes 16777216 | tf_op jit(solution)/shard_map/concatenate | solution.py:43
  45.0 9.0 %fusion.1 = bf16[16384,256]{1,0:T(8,128)(2,1)} fusion(bf16[16384,256]{1,0:T(8,128)(2,1)} %bitcast.98, bf16[1,256,256]{2,1,0:T(8,128)(2,1)S(1)} %copy-done.4), kind=kOutput, calls=%fused_computation.7 | convolution fusion | flops 2155872256 | bytes 16908288 | tf_op jit(solution)/shard_map/dot_general | solution.py:42
  54.0 14.6 %reshape.81 = bf16[512,4,2048]{2,1,0:T(4,128)(2,1)} reshape(bf16[16384,256]{1,0:T(8,128)(2,1)} %fusion.1) | data formatting | bytes 16777216 | tf_op jit(solution)/shard_map/reshape | solution.py:50
  68.5 13.7 %copy.31 = bf16[512,4,2048]{0,2,1:T(8,128)(2,1)} copy(bf16[512,4,2048]{2,1,0:T(4,128)(2,1)} %reshape.81) | data formatting | bytes 16777216 | tf_op jit(solution)/shard_map/reshape | solution.py:50
  82.2 4.6 fusion.73
  86.8 3.8 collective-permute-start.2
  90.5 1.3 collective-permute-start.3
  92.0 42.4 %collective-permute-done.2 = bf16[512,1,2048]{0,2,1:T(8,128)(2,1)S(1)} collective-permute-done((bf16[512,1,2048]{0,2,1:T(8,128)(2,1)}, bf16[512,1,2048]{0,2,1:T(8,128)(2,1)S(1)}, u32[]{:S(2)}, u32[]{:S(2)}) %collective-permute-start.2) | collective-permute-done | bytes 2097184 | tf_op jit(solution)/shard_map/ppermute | solution.py:18
  134.5 4.2 collective-permute-done.3
  138.7 11.7 %fusion.6 = bf16[512,6,2560]{0,2,1:T(8,128)(2,1)S(1)} fusion(bf16[512,1,2048]{0,2,1:T(8,128)(2,1)} %collective-permute-done.3, bf16[512,4,2048]{0,2,1:T(8,128)(2,1)} %copy.31, bf16[512,1,2048]{0,2,1:T(8,128)(2,1)S(1)} %collective-permute-done.2), kind=kLoop, calls=%fused_computation.12 | loop fusion | flops 94371840 | bytes 28311552 | tf_op jit(solution)/shard_map/concatenate | solution.py:20
  150.4 8.6 %fusion.72 = (bf16[512,6,4,512]{0,3,2,1:T(8,128)(2,1)}, bf16[512,6,4,512]{0,3,2,1:T(8,128)(2,1)}) fusion(bf16[512,6,5,512]{0,3,2,1:T(8,128)(2,1)S(1)} %bitcast.97), kind=kLoop, calls=%fused_computation.121 | loop fusion | bytes 50331648 | tf_op jit(solution)/shard_map/slice | solution.py:29
  159.0 20.2 %pad_maximum_fusion = bf16[512,6,4,1024]{0,3,2,1:T(8,128)(2,1)} fusion(bf16[512,6,4,512]{0,3,2,1:T(8,128)(2,1)} %get-tuple-element.26, bf16[512,6,4,512]{0,3,2,1:T(8,128)(2,1)} %get-tuple-element.25), kind=kLoop, calls=%fused_computation.5 | loop fusion | flops 50331648 | bytes 50331648 | tf_op jit(solution)/shard_map/concatenate | solution.py:29
  179.2 22.9 %fusion.71 = (bf16[512,2,4,1024]{0,3,2,1:T(8,128)(2,1)}, bf16[512,2,4,1024]{0,3,2,1:T(8,128)(2,1)}, bf16[512,2,4,1024]{0,3,2,1:T(8,128)(2,1)}, bf16[512,2,4,1024]{0,3,2,1:T(8,128)(2,1)}) fusion(bf16[512,6,4,1024]{0,3,2,1:T(8,128)(2,1)} %pad_maximum_fusion), kind=kLoop, calls=%fused_computation.120 | loop fusion | bytes 67108864 | tf_op jit(solution)/shard_map/slice | solution.py:32
  202.1 14.9 %copy.34 = bf16[512,2,4,1024]{3,2,1,0:T(4,128)(2,1)} copy(bf16[512,2,4,1024]{0,3,2,1:T(8,128)(2,1)} %get-tuple-element.24) | data formatting | bytes 16777216 | tf_op jit(solution)/shard_map/slice | solution.py:32
  217.0 12.6 %reshape.83 = bf16[4096,1024]{1,0:T(8,128)(2,1)} reshape(bf16[512,2,4,1024]{3,2,1,0:T(4,128)(2,1)} %copy.34) | data formatting | bytes 16777216 | tf_op jit(solution)/shard_map/reshape | solution.py:37
  229.5 14.9 %copy.35 = bf16[512,2,4,1024]{3,2,1,0:T(4,128)(2,1)} copy(bf16[512,2,4,1024]{0,3,2,1:T(8,128)(2,1)} %get-tuple-element.23) | data formatting | bytes 16777216 | tf_op jit(solution)/shard_map/slice | solution.py:32
  244.4 12.5 %reshape.84 = bf16[4096,1024]{1,0:T(8,128)(2,1)} reshape(bf16[512,2,4,1024]{3,2,1,0:T(4,128)(2,1)} %copy.35) | data formatting | bytes 16777216 | tf_op jit(solution)/shard_map/reshape | solution.py:37
  256.9 14.9 %copy.36 = bf16[512,2,4,1024]{3,2,1,0:T(4,128)(2,1)} copy(bf16[512,2,4,1024]{0,3,2,1:T(8,128)(2,1)} %get-tuple-element.22) | data formatting | bytes 16777216 | tf_op jit(solution)/shard_map/slice | solution.py:32
  271.8 12.6 %reshape.85 = bf16[4096,1024]{1,0:T(8,128)(2,1)} reshape(bf16[512,2,4,1024]{3,2,1,0:T(4,128)(2,1)} %copy.36) | data formatting | bytes 16777216 | tf_op jit(solution)/shard_map/reshape | solution.py:37
  284.4 14.9 %copy.37 = bf16[512,2,4,1024]{3,2,1,0:T(4,128)(2,1)} copy(bf16[512,2,4,1024]{0,3,2,1:T(8,128)(2,1)} %get-tuple-element.21) | data formatting | bytes 16777216 | tf_op jit(solution)/shard_map/slice | solution.py:32
  299.3 12.8 %reshape.86 = bf16[4096,1024]{1,0:T(8,128)(2,1)} reshape(bf16[512,2,4,1024]{3,2,1,0:T(4,128)(2,1)} %copy.37) | data formatting | bytes 16777216 | tf_op jit(solution)/shard_map/reshape | solution.py:37
  312.1 6.0 fusion.28
  318.1 6.0 convolution_add_fusion.2
  324.1 4.6 convolution_add_fusion.1
  328.7 7.6 fusion.17
  336.3 0.8 bitcast_multiply_fusion
  337.4 41.9 %reduce-scatter.3.cloned.1.call-done = f32[64,256]{1,0:T(8,128)} async-done(((f32[512,256]{1,0:T(8,128)}), f32[64,256]{1,0:T(8,128)}) %reduce-scatter.3.cloned.1.call-update) | async-done | bytes 65552 | tf_op jit(solution)/shard_map/reduce_scatter | solution.py:78
  379.3 1.0 fusion.40
  380.3 0.9 fusion.62
  381.3 73.5 %all-reduce.6.cloned.1.call-done = f32[64,512]{1,0:T(8,128)} async-done(((f32[64,512]{1,0:T(8,128)}), f32[64,512]{1,0:T(8,128)}) %all-reduce.6.cloned.1.call-update) | async-done | bytes 131088 | tf_op jit(solution)/shard_map/psum | solution.py:88
  454.7 1.2 fusion.21
  456.3 30.5 %all_gather.6 = bf16[512,256]{1,0:T(8,128)(2,1)} all-gather(bf16[64,256]{1,0:T(8,128)(2,1)S(1)} %multiply_convert_fusion), channel_id=1, replica_groups=mesh['mod'=16,'sp'=8] {'sp'}, dimensions={0}, use_global_device_ids=true | all-gather | bytes 294912 | tf_op jit(solution)/shard_map/all_gather | solution.py:90
  486.9 54.9 %all-gather.3.cloned.1.call-done = bf16[8192,256]{1,0:T(8,128)(2,1)} async-done(((bf16[512,256]{1,0:T(8,128)(2,1)}), bf16[8192,256]{1,0:T(8,128)(2,1)}) %all-gather.3.cloned.1.call-update) | async-done | bytes 4194320 | tf_op jit(solution)/shard_map/all_gather | solution.py:94
  541.8 5.5 fusion.36
  547.3 0.6 all-reduce.8.cloned.1.call-update
  548.3 139.6 %all-reduce.8.cloned.1.call-done = bf16[512,256]{1,0:T(8,128)(2,1)} async-done(((bf16[512,256]{1,0:T(8,128)(2,1)}), bf16[512,256]{1,0:T(8,128)(2,1)}) %all-reduce.8.cloned.1.call-update) | async-done | bytes 262160 | tf_op jit(solution)/shard_map/psum | solution.py:93
  687.9 2.0 convolution_multiply_fusion
  690.1 11.7 %cholesky.49 = f32[128,128]{1,0:T(8,128)S(1)} custom-call(f32[128,128]{1,0:T(8,128)S(1)} %cholesky.115), custom_call_target="Cholesky" | custom-call | tf_op jit(solution)/shard_map/jit(cholesky)/cholesky | solution.py:100
  701.9 9.8 %custom-call.15 = f32[1,128,128]{1,2,0:T(8,128)S(1)} custom-call(f32[1,128,128]{2,1,0:T(8,128)S(1)} %get-tuple-element.42), custom_call_target="InvertDiagBlocksLowerTriangular" | custom-call | tf_op jit(solution)/shard_map/jit(cholesky)/cholesky | solution.py:100
  711.9 0.3 convolution_subtract_fusion.1
  712.2 11.7 %cholesky.103 = f32[128,128]{1,0:T(8,128)S(1)} custom-call(f32[128,128]{1,0:T(8,128)S(1)} %convolution_subtract_fusion.1), custom_call_target="Cholesky" | custom-call | tf_op jit(solution)/shard_map/jit(cholesky)/cholesky | solution.py:100
  723.9 0.6 compare_reduce_fusion
  726.0 4.2 while.1
  726.3 0.6 fusion.92
  726.8 1.4 bitcast_dynamic-update-slice_fusion.2
  728.3 0.6 fusion.92
  728.8 1.4 bitcast_dynamic-update-slice_fusion.2
  730.2 19.7 %custom-call.16 = f32[2,128,128]{1,2,0:T(8,128)S(1)} custom-call(f32[2,128,128]{2,1,0:T(8,128)S(1)} %get-tuple-element.10), custom_call_target="InvertDiagBlocksLowerTriangular" | custom-call | tf_op jit(solution)/shard_map/jit(_solve_triangular)/triangular_solve | solution.py:102
  749.9 1.0 convert_multiply_fusion
  751.6 4.3 fusion.23
  755.9 0.7 fusion.45
  756.6 1.0 convolution_convert_fusion
  757.6 39.3 %reduce-scatter.5.cloned.1.call-done = bf16[64,256]{1,0:T(8,128)(2,1)} async-done(((bf16[512,256]{1,0:T(8,128)(2,1)}), bf16[64,256]{1,0:T(8,128)(2,1)}) %reduce-scatter.5.cloned.1.call-update) | async-done | bytes 32784 | tf_op jit(solution)/shard_map/reduce_scatter | solution.py:107
  797.0 1.4 bitcast_convert_fusion
  (59 shorter events, 2.6 us)
Async XLA Ops:
  7.2 372.1 %copy-start = (bf16[1,256,512]{2,1,0:T(8,128)(2,1)S(1)}, bf16[1,256,512]{2,1,0:T(8,128)(2,1)}, u32[]{:S(2)}) copy-start(bf16[1,256,512]{2,1,0:T(8,128)(2,1)} %param.10) | copy-start | bytes 786436
  7.2 372.1 %reduce-scatter.3.cloned.1.call-start = ((), (), s32[]{:S(2)}) async-start(), calls=%async_computation.2 | async-start | bytes 589824 | tf_op jit(solution)/shard_map/reduce_scatter | solution.py:78
  10.3 9.5 %collective-permute-start = (bf16[512,1,256]{0,2,1:T(8,128)(2,1)S(1)}, bf16[512,1,256]{0,2,1:T(8,128)(2,1)S(1)}, u32[]{:S(2)}, u32[]{:S(2)}) collective-permute-start(bf16[512,1,256]{0,2,1:T(8,128)(2,1)S(1)} %get-tuple-element.35), channel_id=1, source_target_pairs={{0,1},{1,2},{2,3},{3,4},{4,5},{5,6},{6,7},{8,9},{9,10},{10,11},{11... | collective-permute-start | bytes 786440 | tf_op jit(solution)/shard_map/ppermute | solution.py:18
  14.3 9.8 %collective-permute-start.1 = (bf16[512,1,256]{0,2,1:T(8,128)(2,1)S(1)}, bf16[512,1,256]{0,2,1:T(8,128)(2,1)S(1)}, u32[]{:S(2)}, u32[]{:S(2)}) collective-permute-start(bf16[512,1,256]{0,2,1:T(8,128)(2,1)S(1)} %get-tuple-element.36), channel_id=1, source_target_pairs={{1,0},{2,1},{3,2},{4,3},{5,4},{6,5},{7,6},{9,8},{10,9},{11,10},{12... | collective-permute-start | bytes 786440 | tf_op jit(solution)/shard_map/ppermute | solution.py:19
  30.3 14.7 %copy-start.4 = (bf16[1,256,256]{2,1,0:T(8,128)(2,1)S(1)}, bf16[1,256,256]{2,1,0:T(8,128)(2,1)}, u32[]{:S(2)}) copy-start(bf16[1,256,256]{2,1,0:T(8,128)(2,1)} %param.8) | copy-start | bytes 393220
  82.2 9.6 %copy-start.5 = (s32[1,512,2,4]{1,3,2,0:T(4,128)S(1)}, s32[1,512,2,4]{1,3,2,0:T(4,128)}, u32[]{:S(2)}) copy-start(s32[1,512,2,4]{1,3,2,0:T(4,128)} %param.12) | copy-start | bytes 49156
  86.8 47.7 %collective-permute-start.2 = (bf16[512,1,2048]{0,2,1:T(8,128)(2,1)}, bf16[512,1,2048]{0,2,1:T(8,128)(2,1)S(1)}, u32[]{:S(2)}, u32[]{:S(2)}) collective-permute-start(bf16[512,1,2048]{0,2,1:T(8,128)(2,1)} %get-tuple-element.27), channel_id=1, source_target_pairs={{0,1},{1,2},{2,3},{3,4},{4,5},{5,6},{6,7},{8,9},{9,10},{10,11},{11... | collective-permute-start | bytes 6291464 | tf_op jit(solution)/shard_map/ppermute | solution.py:18
  90.5 48.2 %collective-permute-start.3 = (bf16[512,1,2048]{0,2,1:T(8,128)(2,1)}, bf16[512,1,2048]{0,2,1:T(8,128)(2,1)}, u32[]{:S(2)}, u32[]{:S(2)}) collective-permute-start(bf16[512,1,2048]{0,2,1:T(8,128)(2,1)} %get-tuple-element.28), channel_id=1, source_target_pairs={{1,0},{2,1},{3,2},{4,3},{5,4},{6,5},{7,6},{9,8},{10,9},{11,10},{12... | collective-permute-start | bytes 6291464 | tf_op jit(solution)/shard_map/ppermute | solution.py:19
  299.3 12.8 %copy-start.1 = (bf16[1,4096,256]{2,1,0:T(8,128)(2,1)S(1)}, bf16[1,4096,256]{2,1,0:T(8,128)(2,1)}, u32[]{:S(2)}) copy-start(bf16[1,4096,256]{2,1,0:T(8,128)(2,1)} %param.9) | copy-start | bytes 6291460
  312.1 12.0 %slice-start = ((s8[8388608]{0:T(1024)(128)(4,1)}), s8[4194304]{0:T(1024)(128)(4,1)S(1)}, s32[]{:S(2)}) async-start(s8[8388608]{0:T(1024)(128)(4,1)} %bitcast.99), calls=%async_computation.7 | async-start | bytes 8388608
  318.1 6.0 slice-start.1
  328.7 8.6 %copy-start.6 = (s32[512]{0:T(512)S(1)}, s32[512]{0:T(512)}, u32[]{:S(2)}) copy-start(s32[512]{0:T(512)} %param.13) | copy-start | bytes 6148
  328.7 127.3 %copy-start.3 = (bf16[1,512,256]{2,1,0:T(8,128)(2,1)S(1)}, bf16[1,512,256]{2,1,0:T(8,128)(2,1)}, u32[]{:S(2)}) copy-start(bf16[1,512,256]{2,1,0:T(8,128)(2,1)} %param.11) | copy-start | bytes 786436
  337.2 117.5 %all-reduce.6.cloned.1.call-start = ((), (), s32[]{:S(2)}) async-start(), calls=%async_computation.3 | async-start | bytes 262144 | tf_op jit(solution)/shard_map/psum | solution.py:88
  381.2 160.6 %all-gather.3.cloned.1.call-start = ((), (), s32[]{:S(2)}) async-start(), calls=%async_computation.6 | async-start | bytes 4456448 | tf_op jit(solution)/shard_map/all_gather | solution.py:94
  547.3 140.6 %all-reduce.8.cloned.1.call-start = ((), (), s32[]{:S(2)}) async-start(), calls=%async_computation.4 | async-start | bytes 524288 | tf_op jit(solution)/shard_map/psum | solution.py:93
  547.8 249.1 %reduce-scatter.5.cloned.1.call-start = ((), (), s32[]{:S(2)}) async-start(), calls=%async_computation.5 | async-start | bytes 294912 | tf_op jit(solution)/shard_map/reduce_scatter | solution.py:107
  751.6 46.8 %copy-start.2 = (f32[64,256]{1,0:T(8,128)}, f32[64,256]{1,0:T(8,128)S(1)}, u32[]{:S(2)}) copy-start(f32[64,256]{1,0:T(8,128)S(1)} %maximum_bitcast_fusion) | copy-start | bytes 196612
Sparse Core Ops, SparseCore 0:
  337.3 41.8 reduce-scatter.2
  381.7 72.9 all-reduce.5
  487.0 54.7 all-gather.2
  550.2 137.5 all-reduce.7
  757.8 39.1 reduce-scatter.4
where the time goes:
time: 817 us; the launch traced here: 805 us
  waiting for transfers between devices  405 us (50%)
  local copies, waits for them, and re-layouts  198 us (24%)
  other arithmetic  94.3 us (12%)
  matrix products  50.4 us (6%)
  blocking collectives  30.5 us (4%)
  between operations  15.9 us (2%)
  starting transfers between devices  10.7 us (1%)
    psum x1, waiting for transfers between devices, on_device(): lax.psum(view.astype(jnp.float32).astype(jnp.bfloat16), 'mod')  140 us
    slice x6, local copies, waits for them, and re-layouts, stride_conv(): taps = [joined[:, offset:offset + 2 * rows_out:2] for offset in range(4)]  83.5 us
    psum x1, waiting for transfers between devices, on_device(): scene_sums = lax.psum(local_sums, 'sp')  73.5 us
    all_gather x1, waiting for transfers between devices, on_device(): piece = lax.all_gather(view[None], 'mod', axis=0, tiled=True)  54.9 us
    reshape x4, local copies, waits for them, and re-layouts, stride_conv(): taps[offset].reshape(-1, span)  50.4 us
    ppermute x2, waiting for transfers between devices, extended(): before = lax.ppermute(last, axis, up)  46.6 us
    reduce_scatter x1, waiting for transfers between devices, on_device(): lax.psum_scatter(pooled_part, 'sp', scatter_dimension=0, tiled=True)  41.9 us
    reduce_scatter x1, waiting for transfers between devices, on_device(): lax.psum_scatter(jnp.dot(panel_rows.T, grad_raw, preferred_element_type=j...  39.3 us
  transfers between devices with their start and end apart: 9, of which 9 were waited for; matrix products, arithmetic and copies ran while one was open for 0% of the time, Pallas kernels for 0%

commit v1 on v0

v1 whole, which is shorter than its diff:
```python
import jax
import jax.numpy as jnp
from jax import lax
from jax.experimental import pallas as pl
from jax.experimental.pallas import tpu as pltpu
from jax.sharding import PartitionSpec as P

BANDS = 16
CH = 256
SCENES = 64
HALO = 3


def conv_kernel(edge_ref, x_ref, up_ref, dn_ref, w1_ref, w2_ref, mask_ref, out_ref, band_ref, first_ref):
    samples = x_ref.shape[1]
    rows = x_ref.shape[0]
    cells = mask_ref.shape[1]
    window = 4 * BANDS
    groups = ((0, (0, 1, 2)), (64, (3, 4)), (128, (5, 6, 7)))
    band_ref[...] = jnp.zeros_like(band_ref)
    for start, columns in groups:
        for column in columns:
            low = 2 * BANDS * column - BANDS
            begin, end = (max(low, 0), min(low + window, 256))
            for tap in range(4):
                band_ref[
                    tap * 128 + begin - start : tap * 128 + end - start,
                    column * CH : (column + 1) * CH,
                ] = w1_ref[tap * window + begin - low : tap * window + end - low, :]

    def image_row(row):
        if row < 0:
            return up_ref.at[row + HALO]
        if row >= rows:
            return dn_ref.at[row - rows]
        return x_ref.at[row]

    out_rows = rows // 2
    for row in range(-1, out_rows + 1):
        taps = [image_row(2 * row + tap - 1) for tap in range(4)]
        for start, columns in groups:
            left = jnp.concatenate([tap[:, start : start + 128] for tap in taps], axis=1)
            lanes = slice(columns[0] * CH, (columns[-1] + 1) * CH)
            total = jnp.dot(left, band_ref[:, lanes], preferred_element_type=jnp.float32)
            total = jnp.maximum(total, 0.0)
            if row == -1:
                total = total * edge_ref[0]
            if row == out_rows:
                total = total * edge_ref[1]
            first_ref[row + 1, :, lanes] = total.astype(jnp.bfloat16)
    pooled = jnp.zeros((samples, CH), jnp.float32)
    for row in range(out_rows // 2):
        for column in range(4):
            low, high = (max(2 * column - 1, 0), min(2 * column + 3, 8))
            skip = low - (2 * column - 1)
            total = None
            for tap in range(4):
                part = jnp.dot(
                    first_ref[2 * row + tap, :, low * CH : high * CH],
                    w2_ref[(tap * 4 + skip) * CH : (tap * 4 + skip + high - low) * CH, :],
                    preferred_element_type=jnp.float32,
                )
                total = part if total is None else total + part
            pixel = jnp.maximum(total, 0.0).astype(jnp.bfloat16).astype(jnp.float32)
            cell = row * 4 + column
            pooled = pooled + pixel * mask_ref[:, cell : cell + 1]
    out_ref[...] = pooled


def encode(edge, x, up, dn, w1, w2, mask):
    samples = x.shape[1]
    vmem = pl.BlockSpec(memory_space=pltpu.VMEM)
    return pl.pallas_call(
        conv_kernel,
        out_shape=jax.ShapeDtypeStruct((samples, CH), jnp.float32),
        in_specs=[pl.BlockSpec(memory_space=pltpu.SMEM)] + [vmem] * 6,
        out_specs=vmem,
        scratch_shapes=[
            pltpu.VMEM((512, 8 * CH), jnp.bfloat16),
            pltpu.VMEM((x.shape[0] // 2 + 2, samples, 8 * CH), jnp.bfloat16),
        ],
        compiler_params=pltpu.CompilerParams(vmem_limit_bytes=56 * 1024 * 1024),
        name="encode",
    )(edge, x, up, dn, w1, w2, mask)


def swap(x, axis):
    return lax.all_to_all(x, axis, 0, 0, tiled=True)


def spread(x, axis):
    return swap(jnp.broadcast_to(x[None], (lax.axis_size(axis),) + x.shape), axis)


def on_device(images, conv_first, conv_second, project, whiten, valid_mask, scene_index):
    samples = images.shape[1]
    size = lax.axis_size("sp")
    mods = lax.axis_size("mod")
    place = lax.axis_index("sp")
    share = samples // size
    first_row = place * share
    x = jnp.transpose(images[0], (1, 0, 2))
    up = [(i, i + 1) for i in range(size - 1)]
    down = [(j, i) for i, j in up]
    before = lax.ppermute(x[x.shape[0] - HALO :], "sp", up)
    after = lax.ppermute(x[:HALO], "sp", down)
    edge = jnp.stack([place > 0, place < size - 1]).astype(jnp.float32)
    mask_rows = valid_mask[0].reshape(samples, -1).astype(jnp.float32)
    cells = mask_rows.shape[1] * size
    part = encode(edge, x, before, after, conv_first[0], conv_second[0], mask_rows)
    pieces = swap(part.reshape(size, share, CH), "sp")
    pooled_rows = (jnp.sum(pieces, axis=0) / cells).astype(jnp.bfloat16)
    pooled = spread(pooled_rows, "sp").reshape(samples, CH)

    onehot = (scene_index[:, None] == jnp.arange(SCENES, dtype=jnp.int32)[None, :]).astype(
        jnp.float32
    )
    counts = jnp.sum(onehot, axis=0)
    feat = jnp.dot(pooled, project[0], preferred_element_type=jnp.float32)
    sums = jnp.dot(onehot.T, feat, precision=lax.Precision.HIGHEST)
    means = sums / jnp.maximum(counts, 1.0)[:, None]
    panel = (feat - jnp.dot(onehot, means, precision=lax.Precision.HIGHEST)).astype(jnp.bfloat16)
    raw = jnp.dot(panel, whiten[0], preferred_element_type=jnp.float32)
    scale = 1.0 / jnp.sqrt(jnp.mean(raw * raw, axis=-1, keepdims=True) + 1e-05)
    view = (raw * scale).astype(jnp.bfloat16)

    view_rows = lax.dynamic_slice_in_dim(view, first_row, share, 0)
    scale_rows = lax.dynamic_slice_in_dim(scale, first_row, share, 0)
    inner_part = lax.dot_general(
        view_rows, view, (((1,), (1,)), ((), ())), preferred_element_type=jnp.float32
    )
    inner_pieces = swap(inner_part.reshape(mods, share // mods, samples), "mod")
    view_pieces = swap(view.reshape(mods, samples // mods, CH), "mod")
    inner_sum = jnp.sum(inner_pieces, axis=0)
    view_sum = jnp.sum(view_pieces.astype(jnp.float32), axis=0)
    inner_rows = spread(inner_sum, "mod").reshape(share, samples)
    total = spread(view_sum, "mod").reshape(samples, CH)

    eye = jnp.eye(CH, dtype=jnp.float32)
    mean_view = total / mods
    gram = jnp.dot(mean_view.T, mean_view, precision=lax.Precision.HIGHEST) / samples + 0.001 * eye
    lower = jnp.linalg.cholesky(gram)
    total_rows = lax.dynamic_slice_in_dim(total, first_row, share, 0)
    mean_rows = total_rows / mods
    target_rows = jax.scipy.linalg.solve_triangular(lower, mean_rows.T, lower=True).T
    view_f = view_rows.astype(jnp.float32)
    coupling = (
        jnp.dot(inner_rows, view.astype(jnp.float32), precision=lax.Precision.HIGHEST) / samples
        - total_rows
    )
    grad_full = view_f - target_rows + coupling
    inner = jnp.mean(grad_full * view_f, axis=-1, keepdims=True)
    grad_raw = ((grad_full - view_f * inner) * scale_rows).astype(jnp.bfloat16)
    grad_raw_all = spread(grad_raw, "sp").reshape(samples, CH)
    wide = whiten.shape[1] // size
    panel_own = lax.dynamic_slice_in_dim(panel, place * wide, wide, 1)
    grad_w = lax.dot_general(
        panel_own, grad_raw_all, (((0,), (0,)), ((), ())), preferred_element_type=jnp.float32
    )
    return (target_rows, grad_full.astype(jnp.bfloat16)[None], grad_w[None])


def solution(mesh):
    placed = (
        P("mod", None, "sp", None),
        P("mod", None, None),
        P("mod", None, None),
        P("mod", None, None),
        P("mod", None, None),
        P("mod", None, "sp", None),
        P(),
    )
    return jax.shard_map(
        on_device,
        mesh=mesh,
        in_specs=placed,
        out_specs=(P("sp", None), P("mod", "sp", None), P("mod", "sp", None)),
        check_vma=False,
    )
```

time: 817 us -> 210 us (0.26); the launches traced: 805 us -> 209 us
  waiting for transfers between devices: 405 us -> 54.3 us
  local copies, waits for them, and re-layouts: 198 us -> 10.6 us
  matrix products: 50.4 us -> 7.58 us
  other arithmetic: 94.3 us -> 57 us
  Pallas kernels: 0 us -> 17.9 us
  between operations: 15.9 us -> 2.26 us
  starting transfers between devices: 10.7 us -> 20.3 us
  blocking collectives: 30.5 us -> 38.7 us
    psum x2 -> x0, waiting for transfers between devices: 213 us -> none  [the longest x1 140 us: on_device(): lax.psum(view.astype(jnp.float32).astype(jnp.bfloat16), 'mod')]
    slice x10 -> x1, local copies, waits for them, and re-layouts: 97.3 us -> 1.1 us  [on_device(): after = lax.ppermute(x[:HALO], 'sp', down)]
    reduce_scatter x2 -> x0, waiting for transfers between devices: 81.2 us -> none  [the longest x1 41.9 us: on_device(): lax.psum_scatter(pooled_part, 'sp', scatter_dimension=0, tiled=True)]
    reshape x6 -> x2, local copies, waits for them, and re-layouts: 78.7 us -> 0.09 us  [the longest x1 0.05 us: on_device(): inner_rows = spread(inner_sum, 'mod').reshape(share, samples)]
    all_gather x1 -> x0, waiting for transfers between devices: 54.9 us -> none  [on_device(): piece = lax.all_gather(view[None], 'mod', axis=0, tiled=True)]
    dot_general x12 -> x7, matrix products: 47.3 us -> 5.46 us  [the longest x1 1.35 us: on_device(): jnp.dot(inner_rows, view.astype(jnp.float32), precision=lax.Precision.HIG...]
    all_to_all x0 -> x3, blocking collectives: none -> 38.7 us  [swap(): return lax.all_to_all(x, axis, 0, 0, tiled=True)]
    ppermute x4 -> x2, waiting for transfers between devices: 55.2 us -> 18.3 us  [the longest x1 13.5 us: on_device(): before = lax.ppermute(x[x.shape[0] - HALO:], 'sp', up)]
  transfers between devices with their start and end apart: 9 -> 6, of which waited for: 9 -> 6; matrix products, arithmetic and copies ran while one was open for 0% -> 1% of each run, Pallas kernels for 0% -> 0%
where the time goes in v1:
time: 210 us; the launch traced here: 209 us
  other arithmetic  57 us (27%)
  waiting for transfers between devices  54.3 us (26%)
  blocking collectives  38.7 us (18%)
  starting transfers between devices  20.3 us (10%)
  Pallas kernels  17.9 us (9%)
  local copies, waits for them, and re-layouts  10.6 us (5%)
  matrix products  7.58 us (4%)
  between operations  2.26 us (1%)
    all_to_all x3, blocking collectives, swap(): return lax.all_to_all(x, axis, 0, 0, tiled=True)  38.7 us
    all_to_all x4, waiting for transfers between devices, swap(): return lax.all_to_all(x, axis, 0, 0, tiled=True)  36 us
    another operation x6, other arithmetic, on_device(): lower = jnp.linalg.cholesky(gram)  33.9 us
    another operation x3, other arithmetic, on_device(): jax.scipy.linalg.solve_triangular(lower, mean_rows.T, lower=True)  19.9 us
    pallas_call x1, Pallas kernels, encode(): pl.pallas_call(conv_kernel, out_shape=jax.ShapeDtypeStruct((samples, CH),...  17.9 us
    all_to_all x4, starting transfers between devices, swap(): return lax.all_to_all(x, axis, 0, 0, tiled=True)  14.2 us
    ppermute x1, waiting for transfers between devices, on_device(): before = lax.ppermute(x[x.shape[0] - HALO:], 'sp', up)  13.5 us
    ppermute x1, starting transfers between devices, on_device(): before = lax.ppermute(x[x.shape[0] - HALO:], 'sp', up)  4.84 us
  transfers between devices with their start and end apart: 6, of which 6 were waited for; matrix products, arithmetic and copies ran while one was open for 1% of the time, Pallas kernels for 0%

profile of v1, /device:TPU:0, one launch (start us, length us, event | category | flops | bytes accessed | tf_op | source)
XLA Modules:
  0.0 208.6 jit_solution(13778037630357397706)
XLA Ops:
  0.6 0.0 copy-start
  0.6 2.1 copy.20
  2.7 0.0 copy-start.1
  2.7 0.0 copy-start.4
  2.7 1.1 fusion.30
  3.8 4.8 %collective-permute-start = (bf16[3,512,256]{2,1,0:T(8,128)(2,1)}, bf16[3,512,256]{2,1,0:T(8,128)(2,1)}, u32[]{:S(2)}, u32[]{:S(2)}) collective-permute-start(bf16[3,512,256]{2,1,0:T(8,128)(2,1)} %get-tuple-element.22), channel_id=1, source_target_pairs={{0,1},{1,2},{2,3},{3,4},{4,5},{5,6},{6,7},{8,9},{9,10},{10,11},{11... | collective-permute-start | bytes 2359304 | tf_op jit(solution)/shard_map/ppermute | solution.py:105
  8.7 1.3 collective-permute-start.1
  10.0 0.0 copy-done.4
  10.0 0.8 copy.17.mask_ref
  10.8 0.6 add_convert_fusion.edge_ref
  11.4 13.5 %collective-permute-done.up_ref = bf16[3,512,256]{2,1,0:T(8,128)(2,1)} collective-permute-done((bf16[3,512,256]{2,1,0:T(8,128)(2,1)}, bf16[3,512,256]{2,1,0:T(8,128)(2,1)}, u32[]{:S(2)}, u32[]{:S(2)}) %collective-permute-start) | collective-permute-done | bytes 786464 | tf_op jit(solution)/shard_map/ppermute | solution.py:105
  24.9 4.8 %collective-permute-done.1.dn_ref = bf16[3,512,256]{2,1,0:T(8,128)(2,1)} collective-permute-done((bf16[3,512,256]{2,1,0:T(8,128)(2,1)S(1)}, bf16[3,512,256]{2,1,0:T(8,128)(2,1)}, u32[]{:S(2)}, u32[]{:S(2)}) %collective-permute-start.1) | collective-permute-done | bytes 786464 | tf_op jit(solution)/shard_map/ppermute | solution.py:106
  29.7 0.0 copy-done.1
  29.7 17.9 %encode.1 = f32[512,256]{1,0:T(8,128)} custom-call(f32[2]{0:T(128)} %add_convert_fusion.edge_ref, bf16[8,512,256]{2,1,0:T(8,128)(2,1)} %bitcast.73, bf16[3,512,256]{2,1,0:T(8,128)(2,1)} %collective-permute-done.up_ref, bf16[3,512,256]{2,1,0:T(8,128)(2,1)} %collective-permute-done.1.dn_ref, bf16[256,256]{1,0:T(8,128)(2,1)} %bitcast.81, ...), custom_call_target="tpu_custom_call" | custom-call | tf_op jit(solution)/shard_map/encode/pallas_call | solution.py:73
  47.5 0.0 copy-start.3
  47.5 14.0 %all_to_all.35 = f32[8,64,256]{2,1,0:T(8,128)S(1)} all-to-all(f32[8,64,256]{2,1,0:T(8,128)} %bitcast.75), channel_id=1, replica_groups=mesh['mod'=16,'sp'=8] {'sp'}, dimensions={0} | all-to-all | bytes 1048576 | tf_op jit(solution)/shard_map/all_to_all | solution.py:88
  61.6 0.7 broadcast_in_dim.13
  62.3 3.6 %all-to-all-start.1 = ((bf16[8,64,256]{2,1,0:T(8,128)(2,1)}), bf16[8,64,256]{2,1,0:T(8,128)(2,1)S(1)}, u32[]{:S(2)}, u32[]{:S(2)}) async-start(bf16[8,64,256]{2,1,0:T(8,128)(2,1)} %broadcast_in_dim.13), calls=%async_computation.1 | async-start | bytes 524288 | tf_op jit(solution)/shard_map/all_to_all | solution.py:88
  65.9 0.0 copy-done.3
  65.9 0.1 convert_reduce_fusion.1
  66.0 6.8 %all-to-all-done.1 = bf16[8,64,256]{2,1,0:T(8,128)(2,1)S(1)} async-done(((bf16[8,64,256]{2,1,0:T(8,128)(2,1)}), bf16[8,64,256]{2,1,0:T(8,128)(2,1)S(1)}, u32[]{:S(2)}, u32[]{:S(2)}) %all-to-all-start.1) | async-done | bytes 262176 | tf_op jit(solution)/shard_map/all_to_all | solution.py:88
  72.9 0.0 copy-done
  72.9 0.3 fusion.7
  73.2 0.7 convolution_divide_fusion
  73.9 0.7 fusion
  74.6 0.0 copy-done.5
  74.6 0.4 multiply_reduce_fusion
  75.0 0.9 multiply_convert_fusion
  75.9 1.2 fusion.24
  77.1 15.0 %all_to_all.36 = f32[16,4,512]{2,1,0:T(4,128)S(1)} all-to-all(f32[16,4,512]{2,1,0:T(4,128)S(1)} %reshape.91), channel_id=1, replica_groups=mesh['mod'=16,'sp'=8] {'mod'}, dimensions={0} | all-to-all | bytes 262144 | tf_op jit(solution)/shard_map/all_to_all | solution.py:88
  92.2 3.5 %all-to-all-start.2 = ((bf16[16,32,256]{2,1,0:T(8,128)(2,1)}), bf16[16,32,256]{2,1,0:T(8,128)(2,1)S(1)}, u32[]{:S(2)}, u32[]{:S(2)}) async-start(bf16[16,32,256]{2,1,0:T(8,128)(2,1)} %bitcast.11), calls=%async_computation.2 | async-start | bytes 524288 | tf_op jit(solution)/shard_map/all_to_all | solution.py:88
  95.7 9.1 %all-to-all-done.2 = bf16[16,32,256]{2,1,0:T(8,128)(2,1)S(1)} async-done(((bf16[16,32,256]{2,1,0:T(8,128)(2,1)}), bf16[16,32,256]{2,1,0:T(8,128)(2,1)S(1)}, u32[]{:S(2)}, u32[]{:S(2)}) %all-to-all-start.2) | async-done | bytes 262176 | tf_op jit(solution)/shard_map/all_to_all | solution.py:88
  104.8 0.7 broadcast_in_dim.15
  105.5 3.5 %all-to-all-start.5 = ((f32[16,4,512]{2,1,0:T(4,128)}), f32[16,4,512]{2,1,0:T(4,128)S(1)}, u32[]{:S(2)}, u32[]{:S(2)}) async-start(f32[16,4,512]{2,1,0:T(4,128)} %broadcast_in_dim.15), calls=%async_computation.5 | async-start | bytes 262144 | tf_op jit(solution)/shard_map/all_to_all | solution.py:88
  109.1 7.9 %all-to-all-done.5 = f32[16,4,512]{2,1,0:T(4,128)S(1)} async-done(((f32[16,4,512]{2,1,0:T(4,128)}), f32[16,4,512]{2,1,0:T(4,128)S(1)}, u32[]{:S(2)}, u32[]{:S(2)}) %all-to-all-start.5) | async-done | bytes 131104 | tf_op jit(solution)/shard_map/all_to_all | solution.py:88
  117.0 0.8 broadcast_in_dim.14
  117.8 3.6 %all-to-all-start.3 = ((f32[16,32,256]{2,1,0:T(8,128)}), f32[16,32,256]{2,1,0:T(8,128)S(1)}, u32[]{:S(2)}, u32[]{:S(2)}) async-start(f32[16,32,256]{2,1,0:T(8,128)} %broadcast_in_dim.14), calls=%async_computation.3 | async-start | bytes 1048576 | tf_op jit(solution)/shard_map/all_to_all | solution.py:88
  121.4 0.1 dynamic-slice.3
  121.5 12.2 %all-to-all-done.3 = f32[16,32,256]{2,1,0:T(8,128)S(1)} async-done(((f32[16,32,256]{2,1,0:T(8,128)}), f32[16,32,256]{2,1,0:T(8,128)S(1)}, u32[]{:S(2)}, u32[]{:S(2)}) %all-to-all-start.3) | async-done | bytes 524320 | tf_op jit(solution)/shard_map/all_to_all | solution.py:88
  133.7 1.0 fusion.1
  134.7 0.1 copy.18
  134.9 0.1 add_multiply_fusion
  134.9 11.7 %cholesky.49 = f32[128,128]{1,0:T(8,128)S(1)} custom-call(f32[128,128]{1,0:T(8,128)S(1)} %cholesky.115), custom_call_target="Cholesky" | custom-call | tf_op jit(solution)/shard_map/jit(cholesky)/cholesky | solution.py:142
  146.7 9.8 %custom-call.15 = f32[1,128,128]{1,2,0:T(8,128)S(1)} custom-call(f32[1,128,128]{2,1,0:T(8,128)S(1)} %get-tuple-element.28), custom_call_target="InvertDiagBlocksLowerTriangular" | custom-call | tf_op jit(solution)/shard_map/jit(cholesky)/cholesky | solution.py:142
  156.5 0.2 constant_dynamic-update-slice_fusion
  156.7 0.3 convolution_subtract_fusion.1
  157.0 11.7 %cholesky.103 = f32[128,128]{1,0:T(8,128)S(1)} custom-call(f32[128,128]{1,0:T(8,128)S(1)} %convolution_subtract_fusion.1), custom_call_target="Cholesky" | custom-call | tf_op jit(solution)/shard_map/jit(cholesky)/cholesky | solution.py:142
  168.8 0.6 compare_reduce_fusion
  170.7 0.1 triangular_solve.63
  170.8 4.0 %while.1 = (s32[]{:T(128)}, f32[256,256]{1,0:T(8,128)S(1)}, s32[2,2]{1,0:T(2,128)S(1)}, f32[2,128,128]{2,1,0:T(8,128)S(1)}, s32[]{:T(128)}) while((s32[]{:T(128)}, f32[256,256]{1,0:T(8,128)S(1)}, s32[2,2]{1,0:T(2,128)S(1)}, f32[2,128,128]{2,1,0:T(8,128)S(1)}, s32[]{:T(128)}) %tuple.31), condition=%wide.while_cond, body=%wide.while_body.sunk | while | flops 2 | bytes 131181 | solution.py:145
  170.8 0.6 fusion.44
  171.4 1.4 bitcast_dynamic-update-slice_fusion.2
  172.8 0.6 fusion.44
  173.4 1.4 bitcast_dynamic-update-slice_fusion.2
  174.8 19.9 %custom-call.16 = f32[2,128,128]{1,2,0:T(8,128)S(1)} custom-call(f32[2,128,128]{2,1,0:T(8,128)S(1)} %get-tuple-element.10), custom_call_target="InvertDiagBlocksLowerTriangular" | custom-call | tf_op jit(solution)/shard_map/jit(_solve_triangular)/triangular_solve | solution.py:145
  194.7 0.2 fusion.16
  194.9 0.2 convolution_subtract_fusion.2
  195.2 0.2 fusion.15
  195.4 0.0 copy-start.2
  195.4 1.4 fusion.10
  196.8 1.4 fusion.13
  198.2 9.6 %all_to_all.37 = bf16[8,64,256]{2,1,0:T(8,128)(2,1)S(1)} all-to-all(bf16[8,64,256]{2,1,0:T(8,128)(2,1)S(1)} %broadcast_in_dim.18), channel_id=1, replica_groups=mesh['mod'=16,'sp'=8] {'sp'}, dimensions={0} | all-to-all | bytes 524288 | tf_op jit(solution)/shard_map/all_to_all | solution.py:88
  207.8 0.8 convolution_bitcast_fusion.1
  208.6 0.0 copy-done.2
  (24 shorter events, 0.4 us)
Async XLA Ops:
  0.6 72.3 %copy-start = (bf16[1,256,512]{2,1,0:T(8,128)(2,1)S(1)}, bf16[1,256,512]{2,1,0:T(8,128)(2,1)}, u32[]{:S(2)}) copy-start(bf16[1,256,512]{2,1,0:T(8,128)(2,1)} %param.10) | copy-start | bytes 786436
  2.7 27.0 %copy-start.1 = (bf16[1,512,8,256]{3,1,2,0:T(8,128)(2,1)}, bf16[1,512,8,256]{3,1,2,0:T(8,128)(2,1)S(1)}, u32[]{:S(2)}) copy-start(bf16[1,512,8,256]{3,1,2,0:T(8,128)(2,1)S(1)} %copy.20) | copy-start | bytes 6291460
  2.7 7.3 %copy-start.4 = (s32[1,512,2,4]{1,3,2,0:T(4,128)S(1)}, s32[1,512,2,4]{1,3,2,0:T(4,128)}, u32[]{:S(2)}) copy-start(s32[1,512,2,4]{1,3,2,0:T(4,128)} %param.12) | copy-start | bytes 49156
  3.8 21.0 %collective-permute-start = (bf16[3,512,256]{2,1,0:T(8,128)(2,1)}, bf16[3,512,256]{2,1,0:T(8,128)(2,1)}, u32[]{:S(2)}, u32[]{:S(2)}) collective-permute-start(bf16[3,512,256]{2,1,0:T(8,128)(2,1)} %get-tuple-element.22), channel_id=1, source_target_pairs={{0,1},{1,2},{2,3},{3,4},{4,5},{5,6},{6,7},{8,9},{9,10},{10,11},{11... | collective-permute-start | bytes 2359304 | tf_op jit(solution)/shard_map/ppermute | solution.py:105
  8.7 21.0 %collective-permute-start.1 = (bf16[3,512,256]{2,1,0:T(8,128)(2,1)S(1)}, bf16[3,512,256]{2,1,0:T(8,128)(2,1)}, u32[]{:S(2)}, u32[]{:S(2)}) collective-permute-start(bf16[3,512,256]{2,1,0:T(8,128)(2,1)S(1)} %get-tuple-element.21), channel_id=1, source_target_pairs={{1,0},{2,1},{3,2},{4,3},{5,4},{6,5},{7,6},{9,8},{10,9},{11,10},{12... | collective-permute-start | bytes 2359304 | tf_op jit(solution)/shard_map/ppermute | solution.py:106
  47.5 18.4 %copy-start.3 = (s32[512]{0:T(512)S(1)}, s32[512]{0:T(512)}, u32[]{:S(2)}) copy-start(s32[512]{0:T(512)} %param.13) | copy-start | bytes 6148
  62.3 10.6 %all-to-all-start.1 = ((bf16[8,64,256]{2,1,0:T(8,128)(2,1)}), bf16[8,64,256]{2,1,0:T(8,128)(2,1)S(1)}, u32[]{:S(2)}, u32[]{:S(2)}) async-start(bf16[8,64,256]{2,1,0:T(8,128)(2,1)} %broadcast_in_dim.13), calls=%async_computation.1 | async-start | bytes 524288 | tf_op jit(solution)/shard_map/all_to_all | solution.py:88
  72.9 1.7 copy-start.5
  92.2 12.7 %all-to-all-start.2 = ((bf16[16,32,256]{2,1,0:T(8,128)(2,1)}), bf16[16,32,256]{2,1,0:T(8,128)(2,1)S(1)}, u32[]{:S(2)}, u32[]{:S(2)}) async-start(bf16[16,32,256]{2,1,0:T(8,128)(2,1)} %bitcast.11), calls=%async_computation.2 | async-start | bytes 524288 | tf_op jit(solution)/shard_map/all_to_all | solution.py:88
  105.5 11.5 %all-to-all-start.5 = ((f32[16,4,512]{2,1,0:T(4,128)}), f32[16,4,512]{2,1,0:T(4,128)S(1)}, u32[]{:S(2)}, u32[]{:S(2)}) async-start(f32[16,4,512]{2,1,0:T(4,128)} %broadcast_in_dim.15), calls=%async_computation.5 | async-start | bytes 262144 | tf_op jit(solution)/shard_map/all_to_all | solution.py:88
  117.8 15.9 %all-to-all-start.3 = ((f32[16,32,256]{2,1,0:T(8,128)}), f32[16,32,256]{2,1,0:T(8,128)S(1)}, u32[]{:S(2)}, u32[]{:S(2)}) async-start(f32[16,32,256]{2,1,0:T(8,128)} %broadcast_in_dim.14), calls=%async_computation.3 | async-start | bytes 1048576 | tf_op jit(solution)/shard_map/all_to_all | solution.py:88
  195.4 13.2 %copy-start.2 = (f32[64,256]{1,0:T(8,128)}, f32[64,256]{1,0:T(8,128)S(1)}, u32[]{:S(2)}) copy-start(f32[64,256]{1,0:T(8,128)S(1)} %maximum_bitcast_fusion) | copy-start | bytes 196612

commit v2 on v1

--- a/solution.py
+++ b/solution.py
@@ -8,13 +8,13 @@
 BANDS = 16
 CH = 256
 SCENES = 64
-HALO = 3
-
-
-def conv_kernel(edge_ref, x_ref, up_ref, dn_ref, w1_ref, w2_ref, mask_ref, out_ref, band_ref, first_ref):
-    samples = x_ref.shape[1]
-    rows = x_ref.shape[0]
-    cells = mask_ref.shape[1]
+EXTRA = 8
+
+
+def conv_kernel(got_ref, w1_ref, w2_ref, out_ref, padded_ref, band_ref, first_ref):
+    sources = got_ref.shape[0]
+    share = out_ref.shape[0]
+    rows = (got_ref.shape[1] - EXTRA) // share
     window = 4 * BANDS
     groups = ((0, (0, 1, 2)), (64, (3, 4)), (128, (5, 6, 7)))
     band_ref[...] = jnp.zeros_like(band_ref)
@@ -28,60 +28,90 @@
                     column * CH : (column + 1) * CH,
                 ] = w1_ref[tap * window + begin - low : tap * window + end - low, :]
 
-    def image_row(row):
-        if row < 0:
-            return up_ref.at[row + HALO]
-        if row >= rows:
-            return dn_ref.at[row - rows]
-        return x_ref.at[row]
-
-    out_rows = rows // 2
-    for row in range(-1, out_rows + 1):
-        taps = [image_row(2 * row + tap - 1) for tap in range(4)]
+    total_rows = sources * rows
+    blank = jnp.zeros((share, 256), jnp.bfloat16)
+    padded_ref[0, 0] = blank
+    padded_ref[total_rows // 2, 1] = blank
+    for source in range(sources):
+        for row in range(rows):
+            place = source * rows + row + 1
+            padded_ref[place // 2, place % 2] = got_ref[source, row * share : (row + 1) * share, :]
+    blank = jnp.zeros((share, 8 * CH), jnp.bfloat16)
+    first_ref[0, 0] = blank
+    first_ref[total_rows // 4, 1] = blank
+
+    def first_rows(group, carry):
         for start, columns in groups:
-            left = jnp.concatenate([tap[:, start : start + 128] for tap in taps], axis=1)
+            left = jnp.concatenate(
+                [
+                    padded_ref[
+                        pl.ds(group * 8 + tap // 2, 8), tap % 2, :, start : start + 128
+                    ].reshape(8 * share, 128)
+                    for tap in range(4)
+                ],
+                axis=1,
+            )
             lanes = slice(columns[0] * CH, (columns[-1] + 1) * CH)
             total = jnp.dot(left, band_ref[:, lanes], preferred_element_type=jnp.float32)
-            total = jnp.maximum(total, 0.0)
-            if row == -1:
-                total = total * edge_ref[0]
-            if row == out_rows:
-                total = total * edge_ref[1]
-            first_ref[row + 1, :, lanes] = total.astype(jnp.bfloat16)
-    pooled = jnp.zeros((samples, CH), jnp.float32)
-    for row in range(out_rows // 2):
+            total = jnp.maximum(total, 0.0).astype(jnp.bfloat16)
+            for row in range(8):
+                first_ref[group * 4 + (row + 1) // 2, (row + 1) % 2, :, lanes] = total[
+                    row * share : (row + 1) * share
+                ]
+        return carry
+
+    lax.fori_loop(0, total_rows // 16, first_rows, 0)
+
+    span = 8 * share
+    spot = lax.broadcasted_iota(jnp.int32, (share, span), 1) % share
+    mine = spot == lax.broadcasted_iota(jnp.int32, (share, span), 0)
+    pooled = jnp.zeros((share, CH), jnp.float32)
+    for group in range(total_rows // 32):
         for column in range(4):
             low, high = (max(2 * column - 1, 0), min(2 * column + 3, 8))
             skip = low - (2 * column - 1)
             total = None
             for tap in range(4):
+                left = first_ref[
+                    group * 8 + tap // 2 : group * 8 + tap // 2 + 8, tap % 2, :, low * CH : high * CH
+                ]
                 part = jnp.dot(
-                    first_ref[2 * row + tap, :, low * CH : high * CH],
+                    left.reshape(span, (high - low) * CH),
                     w2_ref[(tap * 4 + skip) * CH : (tap * 4 + skip + high - low) * CH, :],
                     preferred_element_type=jnp.float32,
                 )
                 total = part if total is None else total + part
-            pixel = jnp.maximum(total, 0.0).astype(jnp.bfloat16).astype(jnp.float32)
-            cell = row * 4 + column
-            pooled = pooled + pixel * mask_ref[:, cell : cell + 1]
-    out_ref[...] = pooled
-
-
-def encode(edge, x, up, dn, w1, w2, mask):
-    samples = x.shape[1]
+            pixel = jnp.maximum(total, 0.0).astype(jnp.bfloat16)
+            row = rows * share + column
+            valid = jnp.concatenate(
+                [
+                    got_ref[group * 4 + source, row : row + 1, : 2 * share].astype(jnp.float32)
+                    for source in range(4)
+                ],
+                axis=1,
+            )
+            chosen = jnp.where(mine, valid, 0.0).astype(jnp.bfloat16)
+            pooled = pooled + jnp.dot(chosen, pixel, preferred_element_type=jnp.float32)
+    cells = total_rows
+    out_ref[...] = (pooled / cells).astype(jnp.bfloat16)
+
+
+def encode(got, w1, w2, share):
+    rows = got.shape[0] * (got.shape[1] - EXTRA) // share
     vmem = pl.BlockSpec(memory_space=pltpu.VMEM)
     return pl.pallas_call(
         conv_kernel,
-        out_shape=jax.ShapeDtypeStruct((samples, CH), jnp.float32),
-        in_specs=[pl.BlockSpec(memory_space=pltpu.SMEM)] + [vmem] * 6,
+        out_shape=jax.ShapeDtypeStruct((share, CH), jnp.bfloat16),
+        in_specs=[vmem] * 3,
         out_specs=vmem,
         scratch_shapes=[
+            pltpu.VMEM((rows // 2 + 1, 2, share, 256), jnp.bfloat16),
             pltpu.VMEM((512, 8 * CH), jnp.bfloat16),
-            pltpu.VMEM((x.shape[0] // 2 + 2, samples, 8 * CH), jnp.bfloat16),
+            pltpu.VMEM((rows // 4 + 1, 2, share, 8 * CH), jnp.bfloat16),
         ],
         compiler_params=pltpu.CompilerParams(vmem_limit_bytes=56 * 1024 * 1024),
         name="encode",
-    )(edge, x, up, dn, w1, w2, mask)
+    )(got, w1, w2)
 
 
 def swap(x, axis):
@@ -99,17 +129,14 @@
     place = lax.axis_index("sp")
     share = samples // size
     first_row = place * share
-    x = jnp.transpose(images[0], (1, 0, 2))
-    up = [(i, i + 1) for i in range(size - 1)]
-    down = [(j, i) for i, j in up]
-    before = lax.ppermute(x[x.shape[0] - HALO :], "sp", up)
-    after = lax.ppermute(x[:HALO], "sp", down)
-    edge = jnp.stack([place > 0, place < size - 1]).astype(jnp.float32)
-    mask_rows = valid_mask[0].reshape(samples, -1).astype(jnp.float32)
-    cells = mask_rows.shape[1] * size
-    part = encode(edge, x, before, after, conv_first[0], conv_second[0], mask_rows)
-    pieces = swap(part.reshape(size, share, CH), "sp")
-    pooled_rows = (jnp.sum(pieces, axis=0) / cells).astype(jnp.bfloat16)
+    rows = images.shape[2]
+    x = images[0].reshape(size, share, rows, -1).transpose(0, 2, 1, 3)
+    valid = valid_mask[0].reshape(size, share, 2, 4).transpose(0, 3, 2, 1)
+    valid = valid.reshape(size, 4, 2 * share).astype(jnp.bfloat16)
+    valid = jnp.pad(valid, ((0, 0), (0, EXTRA - 4), (0, 256 - 2 * share)))
+    sent = jnp.concatenate([x.reshape(size, rows * share, -1), valid], axis=1)
+    got = swap(sent, "sp")
+    pooled_rows = encode(got, conv_first[0], conv_second[0], share)
     pooled = spread(pooled_rows, "sp").reshape(samples, CH)
 
     onehot = (scene_index[:, None] == jnp.arange(SCENES, dtype=jnp.int32)[None, :]).astype(
@@ -129,12 +156,29 @@
     inner_part = lax.dot_general(
         view_rows, view, (((1,), (1,)), ((), ())), preferred_element_type=jnp.float32
     )
-    inner_pieces = swap(inner_part.reshape(mods, share // mods, samples), "mod")
-    view_pieces = swap(view.reshape(mods, samples // mods, CH), "mod")
-    inner_sum = jnp.sum(inner_pieces, axis=0)
-    view_sum = jnp.sum(view_pieces.astype(jnp.float32), axis=0)
-    inner_rows = spread(inner_sum, "mod").reshape(share, samples)
-    total = spread(view_sum, "mod").reshape(samples, CH)
+    inner_high = inner_part.astype(jnp.bfloat16)
+    inner_low = (inner_part - inner_high.astype(jnp.float32)).astype(jnp.bfloat16)
+    few = share // mods * samples // CH
+    block = samples // mods
+    pieces = jnp.concatenate(
+        [
+            view.reshape(mods, block, CH),
+            inner_high.reshape(mods, few, CH),
+            inner_low.reshape(mods, few, CH),
+        ],
+        axis=1,
+    )
+    pieces = swap(pieces, "mod").astype(jnp.float32)
+    part = jnp.concatenate(
+        [
+            jnp.sum(pieces[:, :block], axis=0),
+            jnp.sum(pieces[:, block : block + few] + pieces[:, block + few :], axis=0),
+        ],
+        axis=0,
+    )
+    sums = spread(part, "mod")
+    total = sums[:, :block].reshape(samples, CH)
+    inner_rows = sums[:, block:].reshape(share, samples)
 
     eye = jnp.eye(CH, dtype=jnp.float32)
     mean_view = total / mods

time: 210 us -> 180 us (0.86)
  waiting for transfers between devices: 54.3 us -> 20.4 us
  blocking collectives: 38.7 us -> 60.9 us
  starting transfers between devices: 20.3 us -> 7.18 us
    all_to_all x3, blocking collectives: 38.7 us -> 60.9 us  [swap(): return lax.all_to_all(x, axis, 0, 0, tiled=True)]
    ppermute x2 -> x0, waiting for transfers between devices: 18.3 us -> none  [the longest x1 13.5 us: on_device(): before = lax.ppermute(x[x.shape[0] - HALO:], 'sp', up)]
    all_to_all x4 -> x2, waiting for transfers between devices: 36 us -> 20.4 us  [swap(): return lax.all_to_all(x, axis, 0, 0, tiled=True)]
    all_to_all x4 -> x2, starting transfers between devices: 14.2 us -> 7.18 us  [swap(): return lax.all_to_all(x, axis, 0, 0, tiled=True)]
    ppermute x2 -> x0, starting transfers between devices: 6.12 us -> none  [the longest x1 4.84 us: on_device(): before = lax.ppermute(x[x.shape[0] - HALO:], 'sp', up)]
    another operation x7 -> x8, local copies, waits for them, and re-layouts: 4.03 us -> 6.21 us
  transfers between devices with their start and end apart: 6 -> 2, of which waited for: 6 -> 2; matrix products, arithmetic and copies ran while one was open for 1% -> 0% of each run, Pallas kernels for 0% -> 0%
where the time goes in v2:
time: 180 us; the launch traced here: 179 us
  blocking collectives  60.9 us (34%)
  other arithmetic  55.2 us (31%)
  waiting for transfers between devices  20.4 us (11%)
  Pallas kernels  18.5 us (10%)
  local copies, waits for them, and re-layouts  9.16 us (5%)
  starting transfers between devices  7.18 us (4%)
  matrix products  5.58 us (3%)
  between operations  2.28 us (1%)
    all_to_all x3, blocking collectives, swap(): return lax.all_to_all(x, axis, 0, 0, tiled=True)  60.9 us
    another operation x6, other arithmetic, on_device(): lower = jnp.linalg.cholesky(gram)  33.9 us
    all_to_all x2, waiting for transfers between devices, swap(): return lax.all_to_all(x, axis, 0, 0, tiled=True)  20.4 us
    another operation x3, other arithmetic, on_device(): jax.scipy.linalg.solve_triangular(lower, mean_rows.T, lower=True)  19.9 us
    pallas_call x1, Pallas kernels, encode(): pl.pallas_call(conv_kernel, out_shape=jax.ShapeDtypeStruct((share, CH), j...  18.5 us
    all_to_all x2, starting transfers between devices, swap(): return lax.all_to_all(x, axis, 0, 0, tiled=True)  7.18 us
    another operation x7, local copies, waits for them, and re-layouts  4.03 us
  transfers between devices with their start and end apart: 2, of which 2 were waited for; matrix products, arithmetic and copies ran while one was open for 0% of the time, Pallas kernels for 0%

profile of v2, /device:TPU:0, one launch (start us, length us, event | category | flops | bytes accessed | tf_op | source)
XLA Modules:
  0.0 179.2 jit_solution(3801325331896619557)
XLA Ops:
  0.6 0.0 copy-start
  0.6 0.0 copy-start.3
  0.7 2.2 %copy.13 = bf16[8,64,8,256]{3,1,2,0:T(8,128)(2,1)S(1)} copy(bf16[8,64,8,256]{3,2,1,0:T(8,128)(2,1)} %bitcast.73) | data formatting | bytes 4194304 | tf_op jit(solution)/shard_map/reshape;squeeze | solution.py:133
  2.8 0.0 copy-done.3
  2.9 0.1 convert_element_type.47
  3.0 0.1 convert_element_type.49
  3.1 0.1 fusion.1
  3.2 34.1 %all_to_all.25.got_ref = bf16[8,520,256]{2,1,0:T(8,128)(2,1)} all-to-all(bf16[8,520,256]{2,1,0:T(8,128)(2,1)S(1)} %fusion.1), channel_id=1, replica_groups=mesh['mod'=16,'sp'=8] {'sp'}, dimensions={0} | all-to-all | bytes 4259840 | tf_op jit(solution)/shard_map/all_to_all | solution.py:118
  37.3 0.0 copy-start.2
  37.3 18.5 %encode.1 = bf16[64,256]{1,0:T(8,128)(2,1)} custom-call(bf16[8,520,256]{2,1,0:T(8,128)(2,1)} %all_to_all.25.got_ref, bf16[256,256]{1,0:T(8,128)(2,1)} %bitcast.80, bf16[4096,256]{1,0:T(8,128)(2,1)} %bitcast.74), custom_call_target="tpu_custom_call" | custom-call | tf_op jit(solution)/shard_map/encode/pallas_call | solution.py:102
  55.8 1.5 broadcast_in_dim.11
  57.3 3.4 %all-to-all-start.1 = ((bf16[8,64,256]{2,1,0:T(8,128)(2,1)}), bf16[8,64,256]{2,1,0:T(8,128)(2,1)S(1)}, u32[]{:S(2)}, u32[]{:S(2)}) async-start(bf16[8,64,256]{2,1,0:T(8,128)(2,1)} %broadcast_in_dim.11), calls=%async_computation.1 | async-start | bytes 524288 | tf_op jit(solution)/shard_map/all_to_all | solution.py:118
  60.7 0.0 copy-done.2
  60.7 0.1 convert_reduce_fusion
  60.8 7.0 %all-to-all-done.1 = bf16[8,64,256]{2,1,0:T(8,128)(2,1)S(1)} async-done(((bf16[8,64,256]{2,1,0:T(8,128)(2,1)}), bf16[8,64,256]{2,1,0:T(8,128)(2,1)S(1)}, u32[]{:S(2)}, u32[]{:S(2)}) %all-to-all-start.1) | async-done | bytes 262176 | tf_op jit(solution)/shard_map/all_to_all | solution.py:118
  67.9 0.0 copy-done
  67.9 0.0 copy-start.4
  67.9 0.3 fusion.9
  68.2 0.7 convolution_divide_fusion
  68.9 0.7 fusion.2
  69.5 0.0 copy-done.4
  69.6 0.4 multiply_reduce_fusion
  70.0 0.1 multiply_convert_fusion
  70.1 0.2 subtract_convert_fusion
  70.5 17.1 %all_to_all.26 = bf16[16,48,256]{2,1,0:T(8,128)(2,1)S(1)} all-to-all(bf16[16,48,256]{2,1,0:T(8,128)(2,1)S(1)} %pad_maximum_fusion), channel_id=1, replica_groups=mesh['mod'=16,'sp'=8] {'mod'}, dimensions={0} | all-to-all | bytes 786432 | tf_op jit(solution)/shard_map/all_to_all | solution.py:118
  87.6 0.1 convert_element_type.56
  87.7 0.9 broadcast_in_dim.12
  88.6 3.8 %all-to-all-start.3 = ((f32[16,40,256]{2,1,0:T(8,128)}), f32[16,40,256]{2,1,0:T(8,128)S(1)}, u32[]{:S(2)}, u32[]{:S(2)}) async-start(f32[16,40,256]{2,1,0:T(8,128)} %broadcast_in_dim.12), calls=%async_computation.3 | async-start | bytes 1310720 | tf_op jit(solution)/shard_map/all_to_all | solution.py:118
  92.4 0.1 dynamic-slice.3
  92.5 13.4 %all-to-all-done.3 = f32[16,40,256]{2,1,0:T(8,128)S(1)} async-done(((f32[16,40,256]{2,1,0:T(8,128)}), f32[16,40,256]{2,1,0:T(8,128)S(1)}, u32[]{:S(2)}, u32[]{:S(2)}) %all-to-all-start.3) | async-done | bytes 655392 | tf_op jit(solution)/shard_map/all_to_all | solution.py:118
  105.9 1.0 fusion.3
  107.0 0.1 copy.15
  107.1 0.1 add_multiply_fusion
  107.2 11.7 %cholesky.49 = f32[128,128]{1,0:T(8,128)S(1)} custom-call(f32[128,128]{1,0:T(8,128)S(1)} %cholesky.115), custom_call_target="Cholesky" | custom-call | tf_op jit(solution)/shard_map/jit(cholesky)/cholesky | solution.py:186
  119.0 9.8 %custom-call.15 = f32[1,128,128]{1,2,0:T(8,128)S(1)} custom-call(f32[1,128,128]{2,1,0:T(8,128)S(1)} %get-tuple-element.28), custom_call_target="InvertDiagBlocksLowerTriangular" | custom-call | tf_op jit(solution)/shard_map/jit(cholesky)/cholesky | solution.py:186
  128.8 0.2 constant_dynamic-update-slice_fusion
  129.0 0.3 convolution_subtract_fusion.1
  129.2 11.7 %cholesky.103 = f32[128,128]{1,0:T(8,128)S(1)} custom-call(f32[128,128]{1,0:T(8,128)S(1)} %convolution_subtract_fusion.1), custom_call_target="Cholesky" | custom-call | tf_op jit(solution)/shard_map/jit(cholesky)/cholesky | solution.py:186
  141.0 0.6 compare_reduce_fusion
  143.0 0.1 triangular_solve.63
  143.0 4.0 %while.1 = (s32[]{:T(128)}, f32[256,256]{1,0:T(8,128)S(1)}, s32[2,2]{1,0:T(2,128)S(1)}, f32[2,128,128]{2,1,0:T(8,128)S(1)}, s32[]{:T(128)}) while((s32[]{:T(128)}, f32[256,256]{1,0:T(8,128)S(1)}, s32[2,2]{1,0:T(2,128)S(1)}, f32[2,128,128]{2,1,0:T(8,128)S(1)}, s32[]{:T(128)}) %tuple.31), condition=%wide.while_cond, body=%wide.while_body.sunk | while | flops 2 | bytes 131181 | solution.py:189
  143.1 0.6 fusion.47
  143.6 1.4 bitcast_dynamic-update-slice_fusion.2
  145.1 0.6 fusion.47
  145.6 1.4 bitcast_dynamic-update-slice_fusion.2
  147.0 19.9 %custom-call.16 = f32[2,128,128]{1,2,0:T(8,128)S(1)} custom-call(f32[2,128,128]{2,1,0:T(8,128)S(1)} %get-tuple-element.10), custom_call_target="InvertDiagBlocksLowerTriangular" | custom-call | tf_op jit(solution)/shard_map/jit(_solve_triangular)/triangular_solve | solution.py:189
  167.0 0.2 fusion.19
  167.2 0.2 convolution_subtract_fusion.2
  167.5 0.2 fusion.18
  167.7 0.0 copy-start.1
  167.7 0.4 fusion.13
  168.1 0.6 fusion.16
  168.8 9.6 %all_to_all.27 = bf16[8,64,256]{2,1,0:T(8,128)(2,1)S(1)} all-to-all(bf16[8,64,256]{2,1,0:T(8,128)(2,1)S(1)} %broadcast_in_dim.15), channel_id=1, replica_groups=mesh['mod'=16,'sp'=8] {'sp'}, dimensions={0} | all-to-all | bytes 524288 | tf_op jit(solution)/shard_map/all_to_all | solution.py:118
  178.4 0.8 convolution_bitcast_fusion.1
  179.2 0.0 copy-done.1
  (26 shorter events, 0.5 us)
Async XLA Ops:
  0.6 67.2 %copy-start = (bf16[1,256,512]{2,1,0:T(8,128)(2,1)S(1)}, bf16[1,256,512]{2,1,0:T(8,128)(2,1)}, u32[]{:S(2)}) copy-start(bf16[1,256,512]{2,1,0:T(8,128)(2,1)} %param.10) | copy-start | bytes 786436
  0.6 2.2 %copy-start.3 = (s32[1,512,2,4]{1,3,2,0:T(4,128)S(1)}, s32[1,512,2,4]{1,3,2,0:T(4,128)}, u32[]{:S(2)}) copy-start(s32[1,512,2,4]{1,3,2,0:T(4,128)} %param.12) | copy-start | bytes 49156
  37.3 23.4 %copy-start.2 = (s32[512]{0:T(512)S(1)}, s32[512]{0:T(512)}, u32[]{:S(2)}) copy-start(s32[512]{0:T(512)} %param.13) | copy-start | bytes 6148
  57.3 10.6 %all-to-all-start.1 = ((bf16[8,64,256]{2,1,0:T(8,128)(2,1)}), bf16[8,64,256]{2,1,0:T(8,128)(2,1)S(1)}, u32[]{:S(2)}, u32[]{:S(2)}) async-start(bf16[8,64,256]{2,1,0:T(8,128)(2,1)} %broadcast_in_dim.11), calls=%async_computation.1 | async-start | bytes 524288 | tf_op jit(solution)/shard_map/all_to_all | solution.py:118
  67.9 1.7 copy-start.4
  88.6 17.3 %all-to-all-start.3 = ((f32[16,40,256]{2,1,0:T(8,128)}), f32[16,40,256]{2,1,0:T(8,128)S(1)}, u32[]{:S(2)}, u32[]{:S(2)}) async-start(f32[16,40,256]{2,1,0:T(8,128)} %broadcast_in_dim.12), calls=%async_computation.3 | async-start | bytes 1310720 | tf_op jit(solution)/shard_map/all_to_all | solution.py:118
  167.7 11.5 %copy-start.1 = (f32[64,256]{1,0:T(8,128)}, f32[64,256]{1,0:T(8,128)S(1)}, u32[]{:S(2)}) copy-start(f32[64,256]{1,0:T(8,128)S(1)} %maximum_bitcast_fusion) | copy-start | bytes 196612

commit v3 on v2

--- a/solution.py
+++ b/solution.py
@@ -9,11 +9,13 @@
 CH = 256
 SCENES = 64
 EXTRA = 8
+TILE = 8
+BLOCK = 64
 
 
 def conv_kernel(got_ref, w1_ref, w2_ref, out_ref, padded_ref, band_ref, first_ref):
     sources = got_ref.shape[0]
-    share = out_ref.shape[0]
+    share = out_ref.shape[1]
     rows = (got_ref.shape[1] - EXTRA) // share
     window = 4 * BANDS
     groups = ((0, (0, 1, 2)), (64, (3, 4)), (128, (5, 6, 7)))
@@ -92,8 +94,10 @@
             )
             chosen = jnp.where(mine, valid, 0.0).astype(jnp.bfloat16)
             pooled = pooled + jnp.dot(chosen, pixel, preferred_element_type=jnp.float32)
-    cells = total_rows
-    out_ref[...] = (pooled / cells).astype(jnp.bfloat16)
+    cells = total_rows // 4 * 4
+    pooled = (pooled / cells).astype(jnp.bfloat16)
+    for source in range(sources):
+        out_ref[source] = pooled
 
 
 def encode(got, w1, w2, share):
@@ -101,7 +105,7 @@
     vmem = pl.BlockSpec(memory_space=pltpu.VMEM)
     return pl.pallas_call(
         conv_kernel,
-        out_shape=jax.ShapeDtypeStruct((share, CH), jnp.bfloat16),
+        out_shape=jax.ShapeDtypeStruct((got.shape[0], share, CH), jnp.bfloat16),
         in_specs=[vmem] * 3,
         out_specs=vmem,
         scratch_shapes=[
@@ -114,6 +118,218 @@
     )(got, w1, w2)
 
 
+def view_kernel(
+    place_ref, pooled_ref, project_ref, whiten_ref, scene_ref, panel_ref, view_ref, scale_ref, out_ref
+):
+    samples = pooled_ref.shape[0]
+    share = scale_ref.shape[0]
+    mods = out_ref.shape[0]
+    block = samples // mods
+    exact = lax.Precision.HIGHEST
+    feat = jnp.dot(pooled_ref[...], project_ref[...], preferred_element_type=jnp.float32)
+    scene = lax.broadcasted_iota(jnp.int32, (SCENES, samples), 0)
+    onehot = jnp.where(scene == scene_ref[...], 1.0, 0.0)
+    counts = jnp.sum(onehot, axis=1, keepdims=True)
+    sums = jnp.dot(onehot, feat, precision=exact, preferred_element_type=jnp.float32)
+    means = sums / jnp.maximum(counts, 1.0)
+    own = lax.dot_general(
+        onehot,
+        means,
+        (((0,), (0,)), ((), ())),
+        precision=exact,
+        preferred_element_type=jnp.float32,
+    )
+    panel = (feat - own).astype(jnp.bfloat16)
+    panel_ref[...] = panel
+    raw = jnp.dot(panel, whiten_ref[...], preferred_element_type=jnp.float32)
+    scale = lax.rsqrt(jnp.mean(raw * raw, axis=-1, keepdims=True) + 1e-05)
+    view = (raw * scale).astype(jnp.bfloat16)
+    view_ref[...] = view
+    out_ref[:, :block, :] = view.reshape(mods, block, CH)
+    rows = pl.ds(pl.multiple_of(place_ref[0] * share, share), share)
+    mine = view_ref[rows, :]
+    raw_rows = jnp.dot(panel_ref[rows, :], whiten_ref[...], preferred_element_type=jnp.float32)
+    scale_rows = lax.rsqrt(jnp.mean(raw_rows * raw_rows, axis=-1, keepdims=True) + 1e-05)
+    scale_ref[...] = jnp.broadcast_to(scale_rows, scale_ref.shape)
+    inner = lax.dot_general(
+        mine, view, (((1,), (1,)), ((), ())), preferred_element_type=jnp.float32
+    )
+    halves = jnp.concatenate([inner[:, :CH], inner[:, CH:]], axis=0).reshape(mods, -1, CH)
+    high = halves.astype(jnp.bfloat16).astype(jnp.float32)
+    out_ref[:, block:, :] = jnp.concatenate([high, halves - high], axis=1).astype(jnp.bfloat16)
+
+
+def make_view(place, pooled, project, whiten, scene, share, mods):
+    samples = pooled.shape[0]
+    half = 2 * share // mods
+    vmem = pl.BlockSpec(memory_space=pltpu.VMEM)
+    return pl.pallas_call(
+        view_kernel,
+        out_shape=(
+            jax.ShapeDtypeStruct((samples, whiten.shape[0]), jnp.bfloat16),
+            jax.ShapeDtypeStruct((samples, CH), jnp.bfloat16),
+            jax.ShapeDtypeStruct((share, CH), jnp.float32),
+            jax.ShapeDtypeStruct((mods, samples // mods + 2 * half, CH), jnp.bfloat16),
+        ),
+        in_specs=[pl.BlockSpec(memory_space=pltpu.SMEM)] + [vmem] * 4,
+        out_specs=(vmem,) * 4,
+        name="view",
+    )(place, pooled, project, whiten, scene)
+
+
+def pivot_inverse(columns):
+    low = {}
+    for j in range(TILE):
+        for i in range(j, TILE):
+            low[i, j] = jnp.broadcast_to(columns[j][i : i + 1, :], (TILE, 128))
+    inverse = {}
+    for j in range(TILE):
+        root = lax.rsqrt(low[j, j])
+        inverse[j, j] = root
+        for i in range(j + 1, TILE):
+            low[i, j] = low[i, j] * root
+        for m in range(j + 1, TILE):
+            for i in range(m, TILE):
+                low[i, m] = low[i, m] - low[i, j] * low[m, j]
+        for m in range(j):
+            total = low[j, m] * inverse[m, m]
+            for p in range(m + 1, j):
+                total = total + low[j, p] * inverse[p, m]
+            inverse[j, m] = -root * total
+    return inverse
+
+
+def factor_block(work_ref, top):
+    tiles = range(top // 128, work_ref.shape[1] // 128)
+    groups = BLOCK // TILE
+    sub = lax.broadcasted_iota(jnp.int32, (TILE, 128), 0)
+    rows = {}
+    for g in range(groups):
+        for t in tiles:
+            rows[g, t] = work_ref[
+                top + g * TILE : top + (g + 1) * TILE, t * 128 : (t + 1) * 128
+            ]
+
+    def lanes(g, tile, lane):
+        return [
+            jnp.broadcast_to(rows[g, tile][:, lane + j : lane + j + 1], (TILE, 128))
+            for j in range(TILE)
+        ]
+
+    for g in range(groups):
+        at = top + g * TILE
+        tile, lane = (at // 128, at % 128)
+        inverse = pivot_inverse(lanes(g, tile, lane))
+        done = {}
+        for j in range(TILE):
+            column = inverse[TILE - 1, j]
+            for i in range(TILE - 2, j - 1, -1):
+                column = jnp.where(sub == i, inverse[i, j], column)
+            if j:
+                column = jnp.where(sub < j, 0.0, column)
+            for t in tiles:
+                if (t + 1) * 128 <= at:
+                    continue
+                part = column * jnp.broadcast_to(rows[g, t][j : j + 1, :], (TILE, 128))
+                done[t] = part if j == 0 else done[t] + part
+        for t in done:
+            work_ref[at : at + TILE, t * 128 : (t + 1) * 128] = done[t]
+        spreads = {
+            (j, t): jnp.broadcast_to(done[t][j : j + 1, :], (TILE, 128))
+            for t in done
+            for j in range(TILE)
+        }
+        for h in range(g + 1, groups):
+            columns = lanes(h, tile, lane)
+            for j in range(TILE):
+                weight = columns[0] * inverse[j, 0]
+                for m in range(1, j + 1):
+                    weight = weight + columns[m] * inverse[j, m]
+                for t in done:
+                    rows[h, t] = rows[h, t] - weight * spreads[j, t]
+
+
+def solve(work_ref):
+    size = work_ref.shape[0]
+    for top in range(0, size, BLOCK):
+        factor_block(work_ref, top)
+        low = top + BLOCK
+        if low < size:
+            start = low // 128 * 128
+            change = lax.dot_general(
+                work_ref[top:low, start:size],
+                work_ref[top:low, start:],
+                (((0,), (0,)), ((), ())),
+                precision=lax.Precision.HIGHEST,
+                preferred_element_type=jnp.float32,
+            )
+            work_ref[low:, start:] = work_ref[low:, start:] - change[low - start :]
+
+
+def tail_kernel(
+    place_ref, sums_ref, view_ref, scale_ref, target_ref, view_grad_ref, raw_grad_ref, work_ref
+):
+    samples, width = view_ref.shape
+    share = scale_ref.shape[0]
+    mods = sums_ref.shape[0]
+    block = samples // mods
+    owners = share // block
+    total = sums_ref[:, :block, :].reshape(samples, width)
+    mine = sums_ref[pl.ds(place_ref[0] * owners, owners), :block, :].reshape(share, width)
+    gram = lax.dot_general(
+        total,
+        total,
+        (((0,), (0,)), ((), ())),
+        precision=lax.Precision.HIGHEST,
+        preferred_element_type=jnp.float32,
+    )
+    shape = (width, width)
+    eye = lax.broadcasted_iota(jnp.int32, shape, 0) == lax.broadcasted_iota(jnp.int32, shape, 1)
+    work_ref[:, :width] = gram / (mods * mods * samples) + jnp.where(eye, 0.001, 0.0)
+    blank = jnp.zeros((128 - share, width), jnp.float32)
+    work_ref[:, width:] = jnp.concatenate([mine / mods, blank], axis=0).T
+    solve(work_ref)
+    target = work_ref[:, width:].T[:share]
+    target_ref[...] = target
+
+    def times(left, right):
+        high = left.astype(jnp.bfloat16)
+        low = (left - high.astype(jnp.float32)).astype(jnp.bfloat16)
+        return jnp.dot(high, right, preferred_element_type=jnp.float32) + jnp.dot(
+            low, right, preferred_element_type=jnp.float32
+        )
+
+    inner = sums_ref[:, block:, :].reshape(2 * share, width)
+    coupling = times(inner[:share], view_ref[:width, :]) + times(inner[share:], view_ref[width:, :])
+    coupling = coupling / samples - mine
+    rows = pl.ds(pl.multiple_of(place_ref[0] * share, share), share)
+    view = view_ref[rows, :].astype(jnp.float32)
+    grad = view - target + coupling
+    view_grad_ref[...] = grad.astype(jnp.bfloat16)
+    mean = jnp.mean(grad * view, axis=-1, keepdims=True)
+    raw_grad = ((grad - view * mean) * scale_ref[...]).astype(jnp.bfloat16)
+    for source in range(raw_grad_ref.shape[0]):
+        raw_grad_ref[source] = raw_grad
+
+
+def finish(place, sums, view, scale, size):
+    width = view.shape[1]
+    share = scale.shape[0]
+    vmem = pl.BlockSpec(memory_space=pltpu.VMEM)
+    return pl.pallas_call(
+        tail_kernel,
+        out_shape=(
+            jax.ShapeDtypeStruct((share, width), jnp.float32),
+            jax.ShapeDtypeStruct((share, width), jnp.bfloat16),
+            jax.ShapeDtypeStruct((size, share, width), jnp.bfloat16),
+        ),
+        in_specs=[pl.BlockSpec(memory_space=pltpu.SMEM)] + [vmem] * 3,
+        out_specs=(vmem,) * 3,
+        scratch_shapes=[pltpu.VMEM((width, width + 128), jnp.float32)],
+        name="finish",
+    )(place, sums, view, scale)
+
+
 def swap(x, axis):
     return lax.all_to_all(x, axis, 0, 0, tiled=True)
 
@@ -128,7 +344,6 @@
     mods = lax.axis_size("mod")
     place = lax.axis_index("sp")
     share = samples // size
-    first_row = place * share
     rows = images.shape[2]
     x = images[0].reshape(size, share, rows, -1).transpose(0, 2, 1, 3)
     valid = valid_mask[0].reshape(size, share, 2, 4).transpose(0, 3, 2, 1)
@@ -136,39 +351,16 @@
     valid = jnp.pad(valid, ((0, 0), (0, EXTRA - 4), (0, 256 - 2 * share)))
     sent = jnp.concatenate([x.reshape(size, rows * share, -1), valid], axis=1)
     got = swap(sent, "sp")
-    pooled_rows = encode(got, conv_first[0], conv_second[0], share)
-    pooled = spread(pooled_rows, "sp").reshape(samples, CH)
-
-    onehot = (scene_index[:, None] == jnp.arange(SCENES, dtype=jnp.int32)[None, :]).astype(
-        jnp.float32
-    )
-    counts = jnp.sum(onehot, axis=0)
-    feat = jnp.dot(pooled, project[0], preferred_element_type=jnp.float32)
-    sums = jnp.dot(onehot.T, feat, precision=lax.Precision.HIGHEST)
-    means = sums / jnp.maximum(counts, 1.0)[:, None]
-    panel = (feat - jnp.dot(onehot, means, precision=lax.Precision.HIGHEST)).astype(jnp.bfloat16)
-    raw = jnp.dot(panel, whiten[0], preferred_element_type=jnp.float32)
-    scale = 1.0 / jnp.sqrt(jnp.mean(raw * raw, axis=-1, keepdims=True) + 1e-05)
-    view = (raw * scale).astype(jnp.bfloat16)
-
-    view_rows = lax.dynamic_slice_in_dim(view, first_row, share, 0)
-    scale_rows = lax.dynamic_slice_in_dim(scale, first_row, share, 0)
-    inner_part = lax.dot_general(
-        view_rows, view, (((1,), (1,)), ((), ())), preferred_element_type=jnp.float32
-    )
-    inner_high = inner_part.astype(jnp.bfloat16)
-    inner_low = (inner_part - inner_high.astype(jnp.float32)).astype(jnp.bfloat16)
-    few = share // mods * samples // CH
+    pooled = encode(got, conv_first[0], conv_second[0], share)
+    pooled = swap(pooled, "sp").reshape(samples, CH)
+
+    spot = place.reshape(1)
+    panel, view, scale_rows, pieces = make_view(
+        spot, pooled, project[0], whiten[0], scene_index.reshape(1, samples), share, mods
+    )
+    pieces = swap(pieces, "mod").astype(jnp.float32)
     block = samples // mods
-    pieces = jnp.concatenate(
-        [
-            view.reshape(mods, block, CH),
-            inner_high.reshape(mods, few, CH),
-            inner_low.reshape(mods, few, CH),
-        ],
-        axis=1,
-    )
-    pieces = swap(pieces, "mod").astype(jnp.float32)
+    few = 2 * share // mods
     part = jnp.concatenate(
         [
             jnp.sum(pieces[:, :block], axis=0),
@@ -177,31 +369,14 @@
         axis=0,
     )
     sums = spread(part, "mod")
-    total = sums[:, :block].reshape(samples, CH)
-    inner_rows = sums[:, block:].reshape(share, samples)
-
-    eye = jnp.eye(CH, dtype=jnp.float32)
-    mean_view = total / mods
-    gram = jnp.dot(mean_view.T, mean_view, precision=lax.Precision.HIGHEST) / samples + 0.001 * eye
-    lower = jnp.linalg.cholesky(gram)
-    total_rows = lax.dynamic_slice_in_dim(total, first_row, share, 0)
-    mean_rows = total_rows / mods
-    target_rows = jax.scipy.linalg.solve_triangular(lower, mean_rows.T, lower=True).T
-    view_f = view_rows.astype(jnp.float32)
-    coupling = (
-        jnp.dot(inner_rows, view.astype(jnp.float32), precision=lax.Precision.HIGHEST) / samples
-        - total_rows
-    )
-    grad_full = view_f - target_rows + coupling
-    inner = jnp.mean(grad_full * view_f, axis=-1, keepdims=True)
-    grad_raw = ((grad_full - view_f * inner) * scale_rows).astype(jnp.bfloat16)
-    grad_raw_all = spread(grad_raw, "sp").reshape(samples, CH)
+    target_rows, view_grad, raw_grad = finish(spot, sums, view, scale_rows, size)
+    raw_grad = swap(raw_grad, "sp").reshape(samples, CH)
     wide = whiten.shape[1] // size
     panel_own = lax.dynamic_slice_in_dim(panel, place * wide, wide, 1)
     grad_w = lax.dot_general(
-        panel_own, grad_raw_all, (((0,), (0,)), ((), ())), preferred_element_type=jnp.float32
-    )
-    return (target_rows, grad_full.astype(jnp.bfloat16)[None], grad_w[None])
+        panel_own, raw_grad, (((0,), (0,)), ((), ())), preferred_element_type=jnp.float32
+    )
+    return (target_rows, view_grad[None], grad_w[None])
 
 
 def solution(mesh):

time: 180 us -> 132 us (0.73)
  other arithmetic: 55.2 us -> 0.28 us
  Pallas kernels: 18.5 us -> 35.9 us
  blocking collectives: 60.9 us -> 68.2 us
  local copies, waits for them, and re-layouts: 9.16 us -> 3.07 us
  waiting for transfers between devices: 20.4 us -> 14.8 us
  matrix products: 5.58 us -> 1.82 us
    another operation x9 -> x0, other arithmetic: 53.9 us -> none  [the longest x6 33.9 us: on_device(): lower = jnp.linalg.cholesky(gram)]
    pallas_call x1 -> x3, Pallas kernels: 18.5 us -> 35.9 us  [the longest x1 18.6 us: encode(): pl.pallas_call(conv_kernel, out_shape=jax.ShapeDtypeStruct((got.shape[0],...]
    all_to_all x3, blocking collectives: 60.9 us -> 68.2 us  [swap(): return lax.all_to_all(x, axis, 0, 0, tiled=True)]
    all_to_all x2, waiting for transfers between devices: 20.4 us -> 14.8 us  [swap(): return lax.all_to_all(x, axis, 0, 0, tiled=True)]
    another operation x10 -> x0, local copies, waits for them, and re-layouts: 4.13 us -> none
    dot_general x8 -> x1, matrix products: 4.5 us -> 1.82 us  [on_device(): lax.dot_general(panel_own, raw_grad, (((0,), (0,)), ((), ())), preferred_...]
    broadcast_in_dim x3 -> x1, local copies, waits for them, and re-layouts: 2.36 us -> 0.04 us  [spread(): jnp.broadcast_to(x[None], (lax.axis_size(axis),) + x.shape)]
where the time goes in v3:
time: 132 us
  blocking collectives  68.2 us (52%)
  Pallas kernels  35.9 us (27%)
  waiting for transfers between devices  14.8 us (11%)
  starting transfers between devices  6.82 us (5%)
  local copies, waits for them, and re-layouts  3.07 us (2%)
  matrix products  1.82 us (1%)
    all_to_all x3, blocking collectives, swap(): return lax.all_to_all(x, axis, 0, 0, tiled=True)  68.2 us
    pallas_call x1, Pallas kernels, encode(): pl.pallas_call(conv_kernel, out_shape=jax.ShapeDtypeStruct((got.shape[0],...  18.6 us
    all_to_all x2, waiting for transfers between devices, swap(): return lax.all_to_all(x, axis, 0, 0, tiled=True)  14.8 us
    pallas_call x1, Pallas kernels, finish(): pl.pallas_call(tail_kernel, out_shape=(jax.ShapeDtypeStruct((share, width...  13.1 us
    all_to_all x2, starting transfers between devices, swap(): return lax.all_to_all(x, axis, 0, 0, tiled=True)  6.82 us
    pallas_call x1, Pallas kernels, make_view(): pl.pallas_call(view_kernel, out_shape=(jax.ShapeDtypeStruct((samples, whi...  4.24 us
  transfers between devices with their start and end apart: 2, of which 2 were waited for; matrix products, arithmetic and copies ran while one was open for 0% of the time, Pallas kernels for 0%

profile of v3, /device:TPU:0, one launch (start us, length us, event | category | flops | bytes accessed | tf_op | source)
XLA Modules:
  0.0 131.7 jit_solution(10040823429801949989)
XLA Ops:
  0.6 0.0 copy-start.1
  0.6 2.1 %copy.10 = bf16[8,64,8,256]{3,1,2,0:T(8,128)(2,1)S(1)} copy(bf16[8,64,8,256]{3,2,1,0:T(8,128)(2,1)} %bitcast.22) | data formatting | bytes 4194304 | tf_op jit(solution)/shard_map/reshape;squeeze | solution.py:348
  2.8 0.0 copy-done.1
  2.8 0.1 convert_element_type.18
  2.9 0.1 convert_element_type.20
  3.0 0.1 fusion.1
  3.1 34.1 %all_to_all.25.got_ref = bf16[8,520,256]{2,1,0:T(8,128)(2,1)} all-to-all(bf16[8,520,256]{2,1,0:T(8,128)(2,1)S(1)} %fusion.1), channel_id=1, replica_groups=mesh['mod'=16,'sp'=8] {'sp'}, dimensions={0} | all-to-all | bytes 4259840 | tf_op jit(solution)/shard_map/all_to_all | solution.py:334
  37.3 18.6 %encode.1 = bf16[8,64,256]{2,1,0:T(8,128)(2,1)} custom-call(bf16[8,520,256]{2,1,0:T(8,128)(2,1)} %all_to_all.25.got_ref, bf16[256,256]{1,0:T(8,128)(2,1)} %bitcast.28, bf16[4096,256]{1,0:T(8,128)(2,1)} %bitcast.23), custom_call_target="tpu_custom_call" | custom-call | tf_op jit(solution)/shard_map/encode/pallas_call | solution.py:106
  55.8 3.4 %all-to-all-start.1 = ((bf16[8,64,256]{2,1,0:T(8,128)(2,1)}), bf16[8,64,256]{2,1,0:T(8,128)(2,1)S(1)}, u32[]{:S(2)}, u32[]{:S(2)}) async-start(bf16[8,64,256]{2,1,0:T(8,128)(2,1)} %encode.1), calls=%async_computation.1 | async-start | bytes 524288 | tf_op jit(solution)/shard_map/all_to_all | solution.py:334
  59.3 7.2 %all-to-all-done.1 = bf16[8,64,256]{2,1,0:T(8,128)(2,1)S(1)} async-done(((bf16[8,64,256]{2,1,0:T(8,128)(2,1)}), bf16[8,64,256]{2,1,0:T(8,128)(2,1)S(1)}, u32[]{:S(2)}, u32[]{:S(2)}) %all-to-all-start.1) | async-done | bytes 262176 | tf_op jit(solution)/shard_map/all_to_all | solution.py:334
  66.4 0.0 copy-start
  66.4 0.7 copy-done
  67.1 4.2 %view.1 = (bf16[512,512]{1,0:T(8,128)(2,1)}, bf16[512,256]{1,0:T(8,128)(2,1)}, f32[64,256]{1,0:T(8,128)}, bf16[16,48,256]{2,1,0:T(8,128)(2,1)}) custom-call(s32[1]{0:T(128)} %bitcast.place_ref, bf16[512,256]{1,0:T(8,128)(2,1)} %bitcast.25, bf16[256,512]{1,0:T(8,128)(2,1)} %bitcast.26, bf16[512,256]{1,0:T(8,128)(2,1)} %bitcast.27, s32[1,512]{1,0:T(1,128)} %bitcast.30), custom_call_target="tpu_custom_call" | custom-call | tf_op jit(solution)/shard_map/view/pallas_call | solution.py:166
  71.4 17.3 %all_to_all.26 = bf16[16,48,256]{2,1,0:T(8,128)(2,1)S(1)} all-to-all(bf16[16,48,256]{2,1,0:T(8,128)(2,1)} %get-tuple-element.10), channel_id=1, replica_groups=mesh['mod'=16,'sp'=8] {'mod'}, dimensions={0} | all-to-all | bytes 786432 | tf_op jit(solution)/shard_map/all_to_all | solution.py:334
  88.7 0.1 convert_element_type.21
  88.9 16.8 %all_to_all.27.sums_ref = f32[16,40,256]{2,1,0:T(8,128)} all-to-all(f32[16,40,256]{2,1,0:T(8,128)S(1)} %broadcast_in_dim.12), channel_id=1, replica_groups=mesh['mod'=16,'sp'=8] {'mod'}, dimensions={0} | all-to-all | bytes 1310720 | tf_op jit(solution)/shard_map/all_to_all | solution.py:334
  105.7 13.1 %finish.1 = (f32[64,256]{1,0:T(8,128)}, bf16[64,256]{1,0:T(8,128)(2,1)}, bf16[8,64,256]{2,1,0:T(8,128)(2,1)}) custom-call(s32[1]{0:T(128)} %bitcast.place_ref, f32[16,40,256]{2,1,0:T(8,128)} %all_to_all.27.sums_ref, bf16[512,256]{1,0:T(8,128)(2,1)} %get-tuple-element.11.view_ref, f32[64,256]{1,0:T(8,128)} %get-tuple-element.12.scale_ref), custom_call_target="tpu_custom_call" | custom-call | tf_op jit(solution)/shard_map/finish/pallas_call | solution.py:319
  118.8 3.4 %all-to-all-start.4 = ((bf16[8,64,256]{2,1,0:T(8,128)(2,1)}), bf16[8,64,256]{2,1,0:T(8,128)(2,1)S(1)}, u32[]{:S(2)}, u32[]{:S(2)}) async-start(bf16[8,64,256]{2,1,0:T(8,128)(2,1)} %get-tuple-element.16), calls=%async_computation.4 | async-start | bytes 524288 | tf_op jit(solution)/shard_map/all_to_all | solution.py:334
  122.2 7.7 %all-to-all-done.4 = bf16[8,64,256]{2,1,0:T(8,128)(2,1)S(1)} async-done(((bf16[8,64,256]{2,1,0:T(8,128)(2,1)}), bf16[8,64,256]{2,1,0:T(8,128)(2,1)S(1)}, u32[]{:S(2)}, u32[]{:S(2)}) %all-to-all-start.4) | async-done | bytes 262176 | tf_op jit(solution)/shard_map/all_to_all | solution.py:334
  129.9 1.8 %convolution_bitcast_fusion = f32[1,64,256]{2,1,0:T(8,128)} fusion(bf16[512,256]{1,0:T(8,128)(2,1)S(1)} %bitcast.24, bf16[512,512]{1,0:T(8,128)(2,1)} %get-tuple-element.15, s32[]{:T(128)S(6)} %select_n.3), kind=kOutput, calls=%fused_computation.3 | convolution fusion | flops 16777216 | bytes 458756 | tf_op jit(solution)/shard_map/dot_general | solution.py:376
  (6 shorter events, 0.1 us)
Async XLA Ops:
  0.6 2.2 %copy-start.1 = (s32[1,512,2,4]{1,3,2,0:T(4,128)S(1)}, s32[1,512,2,4]{1,3,2,0:T(4,128)}, u32[]{:S(2)}) copy-start(s32[1,512,2,4]{1,3,2,0:T(4,128)} %param.12) | copy-start | bytes 49156
  55.8 10.6 %all-to-all-start.1 = ((bf16[8,64,256]{2,1,0:T(8,128)(2,1)}), bf16[8,64,256]{2,1,0:T(8,128)(2,1)S(1)}, u32[]{:S(2)}, u32[]{:S(2)}) async-start(bf16[8,64,256]{2,1,0:T(8,128)(2,1)} %encode.1), calls=%async_computation.1 | async-start | bytes 524288 | tf_op jit(solution)/shard_map/all_to_all | solution.py:334
  66.4 0.7 copy-start
  118.8 11.1 %all-to-all-start.4 = ((bf16[8,64,256]{2,1,0:T(8,128)(2,1)}), bf16[8,64,256]{2,1,0:T(8,128)(2,1)S(1)}, u32[]{:S(2)}, u32[]{:S(2)}) async-start(bf16[8,64,256]{2,1,0:T(8,128)(2,1)} %get-tuple-element.16), calls=%async_computation.4 | async-start | bytes 524288 | tf_op jit(solution)/shard_map/all_to_all | solution.py:334

commit v4 on v3

--- a/solution.py
+++ b/solution.py
@@ -8,6 +8,7 @@
 BANDS = 16
 CH = 256
 SCENES = 64
+MODS = 16
 EXTRA = 8
 TILE = 8
 BLOCK = 64
@@ -119,12 +120,9 @@
 
 
 def view_kernel(
-    place_ref, pooled_ref, project_ref, whiten_ref, scene_ref, panel_ref, view_ref, scale_ref, out_ref
+    place_ref, pooled_ref, project_ref, whiten_ref, scene_ref, columns_ref, view_ref, scale_ref
 ):
     samples = pooled_ref.shape[0]
-    share = scale_ref.shape[0]
-    mods = out_ref.shape[0]
-    block = samples // mods
     exact = lax.Precision.HIGHEST
     feat = jnp.dot(pooled_ref[...], project_ref[...], preferred_element_type=jnp.float32)
     scene = lax.broadcasted_iota(jnp.int32, (SCENES, samples), 0)
@@ -140,41 +138,84 @@
         preferred_element_type=jnp.float32,
     )
     panel = (feat - own).astype(jnp.bfloat16)
-    panel_ref[...] = panel
     raw = jnp.dot(panel, whiten_ref[...], preferred_element_type=jnp.float32)
     scale = lax.rsqrt(jnp.mean(raw * raw, axis=-1, keepdims=True) + 1e-05)
-    view = (raw * scale).astype(jnp.bfloat16)
-    view_ref[...] = view
-    out_ref[:, :block, :] = view.reshape(mods, block, CH)
-    rows = pl.ds(pl.multiple_of(place_ref[0] * share, share), share)
-    mine = view_ref[rows, :]
-    raw_rows = jnp.dot(panel_ref[rows, :], whiten_ref[...], preferred_element_type=jnp.float32)
-    scale_rows = lax.rsqrt(jnp.mean(raw_rows * raw_rows, axis=-1, keepdims=True) + 1e-05)
-    scale_ref[...] = jnp.broadcast_to(scale_rows, scale_ref.shape)
-    inner = lax.dot_general(
-        mine, view, (((1,), (1,)), ((), ())), preferred_element_type=jnp.float32
-    )
-    halves = jnp.concatenate([inner[:, :CH], inner[:, CH:]], axis=0).reshape(mods, -1, CH)
-    high = halves.astype(jnp.bfloat16).astype(jnp.float32)
-    out_ref[:, block:, :] = jnp.concatenate([high, halves - high], axis=1).astype(jnp.bfloat16)
-
-
-def make_view(place, pooled, project, whiten, scene, share, mods):
+    scale_ref[...] = jnp.broadcast_to(scale, scale_ref.shape)
+    view_ref[...] = (raw * scale).astype(jnp.bfloat16)
+    wide, depth = (columns_ref.shape[0], panel.shape[1])
+    feature = lax.broadcasted_iota(jnp.int32, (wide, depth), 1)
+    wanted = lax.broadcasted_iota(jnp.int32, (wide, depth), 0) + place_ref[0] * wide
+    pick = jnp.where(feature == wanted, 1.0, 0.0).astype(jnp.bfloat16)
+    columns = lax.dot_general(
+        pick, panel, (((1,), (1,)), ((), ())), preferred_element_type=jnp.float32
+    )
+    columns_ref[...] = columns.astype(jnp.bfloat16)
+
+
+def make_view(place, pooled, project, whiten, scene, size):
     samples = pooled.shape[0]
-    half = 2 * share // mods
     vmem = pl.BlockSpec(memory_space=pltpu.VMEM)
     return pl.pallas_call(
         view_kernel,
         out_shape=(
-            jax.ShapeDtypeStruct((samples, whiten.shape[0]), jnp.bfloat16),
+            jax.ShapeDtypeStruct((whiten.shape[0] // size, samples), jnp.bfloat16),
             jax.ShapeDtypeStruct((samples, CH), jnp.bfloat16),
-            jax.ShapeDtypeStruct((share, CH), jnp.float32),
-            jax.ShapeDtypeStruct((mods, samples // mods + 2 * half, CH), jnp.bfloat16),
+            jax.ShapeDtypeStruct((samples, 128), jnp.float32),
         ),
         in_specs=[pl.BlockSpec(memory_space=pltpu.SMEM)] + [vmem] * 4,
-        out_specs=(vmem,) * 4,
+        out_specs=(vmem,) * 3,
         name="view",
     )(place, pooled, project, whiten, scene)
+
+
+def pair_kernel(place_ref, view_ref, other_ref, out_ref):
+    chips = out_ref.shape[0]
+    half = view_ref.shape[0] // 2
+    block = half // chips
+    rows = pl.ds(pl.multiple_of(place_ref[1] * half, half), half)
+    first, second = (view_ref[rows, :], other_ref[rows, :])
+    both = first.astype(jnp.float32) + second.astype(jnp.float32)
+    out_ref[:, :block, :] = both.astype(jnp.bfloat16).reshape(chips, block, CH)
+    over = (((1,), (1,)), ((), ()))
+    inner = lax.dot_general(first, view_ref[...], over, preferred_element_type=jnp.float32)
+    inner = inner + lax.dot_general(
+        second, other_ref[...], over, preferred_element_type=jnp.float32
+    )
+    inner = inner.astype(jnp.bfloat16)
+    out_ref[:, block : 2 * block, :] = inner[:, :CH].reshape(chips, block, CH)
+    out_ref[:, 2 * block :, :] = inner[:, CH:].reshape(chips, block, CH)
+
+
+def pair_sums(place, view, other, chips):
+    vmem = pl.BlockSpec(memory_space=pltpu.VMEM)
+    block = view.shape[0] // 2 // chips
+    return pl.pallas_call(
+        pair_kernel,
+        out_shape=jax.ShapeDtypeStruct((chips, 3 * block, CH), jnp.bfloat16),
+        in_specs=[pl.BlockSpec(memory_space=pltpu.SMEM), vmem, vmem],
+        out_specs=vmem,
+        name="pair",
+    )(place, view, other)
+
+
+def sum_kernel(in_ref, out_ref):
+    total = in_ref[0].astype(jnp.float32)
+    for source in range(1, in_ref.shape[0]):
+        total = total + in_ref[source].astype(jnp.float32)
+    total = total.astype(jnp.bfloat16)
+    for source in range(in_ref.shape[0]):
+        out_ref[source] = total
+
+
+def sum_spread(x):
+    vmem = pl.BlockSpec(memory_space=pltpu.VMEM)
+    return pl.pallas_call(
+        sum_kernel,
+        out_shape=jax.ShapeDtypeStruct(x.shape, x.dtype),
+        in_specs=[vmem],
+        out_specs=vmem,
+        name="sums",
+    )(x)
 
 
 def pivot_inverse(columns):
@@ -200,7 +241,8 @@
 
 
 def factor_block(work_ref, top):
-    tiles = range(top // 128, work_ref.shape[1] // 128)
+    half = work_ref.shape[1] // 256
+    tiles = [t for t in range(top // 128, 2 * half) if t < half or (t - half) * 128 <= top]
     groups = BLOCK // TILE
     sub = lax.broadcasted_iota(jnp.int32, (TILE, 128), 0)
     rows = {}
@@ -228,8 +270,6 @@
             if j:
                 column = jnp.where(sub < j, 0.0, column)
             for t in tiles:
-                if (t + 1) * 128 <= at:
-                    continue
                 part = column * jnp.broadcast_to(rows[g, t][j : j + 1, :], (TILE, 128))
                 done[t] = part if j == 0 else done[t] + part
         for t in done:
@@ -267,75 +307,89 @@
 
 
 def tail_kernel(
-    place_ref, sums_ref, view_ref, scale_ref, target_ref, view_grad_ref, raw_grad_ref, work_ref
+    place_ref,
+    sums_ref,
+    other_ref,
+    view_ref,
+    scale_ref,
+    columns_ref,
+    target_ref,
+    view_grad_ref,
+    weight_grad_ref,
+    work_ref,
+    full_ref,
 ):
     samples, width = view_ref.shape
-    share = scale_ref.shape[0]
-    mods = sums_ref.shape[0]
-    block = samples // mods
-    owners = share // block
-    total = sums_ref[:, :block, :].reshape(samples, width)
-    mine = sums_ref[pl.ds(place_ref[0] * owners, owners), :block, :].reshape(share, width)
+    share = target_ref.shape[0]
+    block = sums_ref.shape[1] // 3
+    half = samples // 2
+    core = place_ref[1]
+
+    def whole(part):
+        lanes = slice(part * block, (part + 1) * block)
+        mine = sums_ref[:, lanes, :].reshape(half, width)
+        other = other_ref[:, lanes, :].reshape(half, width)
+        return jnp.concatenate(
+            [jnp.where(core == 0, mine, other), jnp.where(core == 0, other, mine)], axis=0
+        )
+
+    total = whole(0)
+    mean = total * (1.0 / MODS)
     gram = lax.dot_general(
-        total,
-        total,
-        (((0,), (0,)), ((), ())),
+        mean, mean, (((0,), (0,)), ((), ())), preferred_element_type=jnp.float32
+    )
+    shape = (width, width)
+    eye = lax.broadcasted_iota(jnp.int32, shape, 0) == lax.broadcasted_iota(jnp.int32, shape, 1)
+    work_ref[:, :width] = gram / samples + jnp.where(eye, 0.001, 0.0)
+    work_ref[:, width:] = jnp.where(eye, 1.0, 0.0)
+    solve(work_ref)
+    target = lax.dot_general(
+        mean.astype(jnp.float32),
+        work_ref[:, width:],
+        (((1,), (1,)), ((), ())),
         precision=lax.Precision.HIGHEST,
         preferred_element_type=jnp.float32,
     )
-    shape = (width, width)
-    eye = lax.broadcasted_iota(jnp.int32, shape, 0) == lax.broadcasted_iota(jnp.int32, shape, 1)
-    work_ref[:, :width] = gram / (mods * mods * samples) + jnp.where(eye, 0.001, 0.0)
-    blank = jnp.zeros((128 - share, width), jnp.float32)
-    work_ref[:, width:] = jnp.concatenate([mine / mods, blank], axis=0).T
-    solve(work_ref)
-    target = work_ref[:, width:].T[:share]
-    target_ref[...] = target
-
-    def times(left, right):
-        high = left.astype(jnp.bfloat16)
-        low = (left - high.astype(jnp.float32)).astype(jnp.bfloat16)
-        return jnp.dot(high, right, preferred_element_type=jnp.float32) + jnp.dot(
-            low, right, preferred_element_type=jnp.float32
-        )
-
-    inner = sums_ref[:, block:, :].reshape(2 * share, width)
-    coupling = times(inner[:share], view_ref[:width, :]) + times(inner[share:], view_ref[width:, :])
-    coupling = coupling / samples - mine
-    rows = pl.ds(pl.multiple_of(place_ref[0] * share, share), share)
-    view = view_ref[rows, :].astype(jnp.float32)
+    coupling = jnp.dot(whole(1), view_ref[:width, :], preferred_element_type=jnp.float32)
+    coupling = coupling + jnp.dot(whole(2), view_ref[width:, :], preferred_element_type=jnp.float32)
+    coupling = coupling / samples - total.astype(jnp.float32)
+    view = view_ref[...].astype(jnp.float32)
     grad = view - target + coupling
-    view_grad_ref[...] = grad.astype(jnp.bfloat16)
-    mean = jnp.mean(grad * view, axis=-1, keepdims=True)
-    raw_grad = ((grad - view * mean) * scale_ref[...]).astype(jnp.bfloat16)
-    for source in range(raw_grad_ref.shape[0]):
-        raw_grad_ref[source] = raw_grad
-
-
-def finish(place, sums, view, scale, size):
-    width = view.shape[1]
-    share = scale.shape[0]
+    share_rows = pl.ds(pl.multiple_of(place_ref[0] * share, share), share)
+    full_ref[...] = target
+    target_ref[...] = full_ref[share_rows, :]
+    full_ref[...] = grad
+    view_grad_ref[...] = full_ref[share_rows, :].astype(jnp.bfloat16)
+    inner = jnp.mean(grad * view, axis=-1, keepdims=True)
+    scale = jnp.concatenate([scale_ref[...]] * (width // 128), axis=1)
+    raw_grad = ((grad - view * inner) * scale).astype(jnp.bfloat16)
+    weight_grad_ref[...] = jnp.dot(
+        columns_ref[...], raw_grad, preferred_element_type=jnp.float32
+    )
+
+
+def finish(place, sums, other, view, scale, columns, share):
+    samples, width = view.shape
     vmem = pl.BlockSpec(memory_space=pltpu.VMEM)
     return pl.pallas_call(
         tail_kernel,
         out_shape=(
             jax.ShapeDtypeStruct((share, width), jnp.float32),
             jax.ShapeDtypeStruct((share, width), jnp.bfloat16),
-            jax.ShapeDtypeStruct((size, share, width), jnp.bfloat16),
+            jax.ShapeDtypeStruct((columns.shape[0], width), jnp.float32),
         ),
-        in_specs=[pl.BlockSpec(memory_space=pltpu.SMEM)] + [vmem] * 3,
+        in_specs=[pl.BlockSpec(memory_space=pltpu.SMEM)] + [vmem] * 5,
         out_specs=(vmem,) * 3,
-        scratch_shapes=[pltpu.VMEM((width, width + 128), jnp.float32)],
+        scratch_shapes=[
+            pltpu.VMEM((width, 2 * width), jnp.float32),
+            pltpu.VMEM((samples, width), jnp.float32),
+        ],
         name="finish",
-    )(place, sums, view, scale)
-
-
-def swap(x, axis):
-    return lax.all_to_all(x, axis, 0, 0, tiled=True)
-
-
-def spread(x, axis):
-    return swap(jnp.broadcast_to(x[None], (lax.axis_size(axis),) + x.shape), axis)
+    )(place, sums, other, view, scale, columns)
+
+
+def swap(x, axis, groups=None):
+    return lax.all_to_all(x, axis, 0, 0, tiled=True, axis_index_groups=groups)
 
 
 def on_device(images, conv_first, conv_second, project, whiten, valid_mask, scene_index):
@@ -354,28 +408,17 @@
     pooled = encode(got, conv_first[0], conv_second[0], share)
     pooled = swap(pooled, "sp").reshape(samples, CH)
 
-    spot = place.reshape(1)
-    panel, view, scale_rows, pieces = make_view(
-        spot, pooled, project[0], whiten[0], scene_index.reshape(1, samples), share, mods
-    )
-    pieces = swap(pieces, "mod").astype(jnp.float32)
-    block = samples // mods
-    few = 2 * share // mods
-    part = jnp.concatenate(
-        [
-            jnp.sum(pieces[:, :block], axis=0),
-            jnp.sum(pieces[:, block : block + few] + pieces[:, block + few :], axis=0),
-        ],
-        axis=0,
-    )
-    sums = spread(part, "mod")
-    target_rows, view_grad, raw_grad = finish(spot, sums, view, scale_rows, size)
-    raw_grad = swap(raw_grad, "sp").reshape(samples, CH)
-    wide = whiten.shape[1] // size
-    panel_own = lax.dynamic_slice_in_dim(panel, place * wide, wide, 1)
-    grad_w = lax.dot_general(
-        panel_own, raw_grad, (((0,), (0,)), ((), ())), preferred_element_type=jnp.float32
-    )
+    spot = jnp.stack([place, lax.axis_index("mod") % 2])
+    columns, view, scale = make_view(
+        spot, pooled, project[0], whiten[0], scene_index.reshape(1, samples), size
+    )
+    partner = [(i, i ^ 1) for i in range(mods)]
+    chips = [[2 * i + core for i in range(mods // 2)] for core in range(2)]
+    pieces = pair_sums(spot, view, lax.ppermute(view, "mod", partner), mods // 2)
+    pieces = sum_spread(swap(pieces, "mod", chips))
+    sums = swap(pieces, "mod", chips)
+    other = lax.ppermute(sums, "mod", partner)
+    target_rows, view_grad, grad_w = finish(spot, sums, other, view, scale, columns, share)
     return (target_rows, view_grad[None], grad_w[None])
 
 

time: 132 us -> 126 us (0.955); the launches traced: 132 us -> 124 us
  waiting for transfers between devices: 14.8 us -> 10 us
  Pallas kernels: 35.9 us -> 40.2 us
  blocking collectives: 68.2 us -> 63.9 us
  starting transfers between devices: 6.82 us -> 3.42 us
  matrix products: 1.82 us -> 0 us
  local copies, waits for them, and re-layouts: 3.07 us -> 4.44 us
    all_to_all x2 -> x1, waiting for transfers between devices: 14.8 us -> 6.56 us  [swap(): return lax.all_to_all(x, axis, 0, 0, tiled=True, axis_index_groups=groups)]
    all_to_all x3, blocking collectives: 68.2 us -> 63.9 us  [swap(): return lax.all_to_all(x, axis, 0, 0, tiled=True, axis_index_groups=groups)]
    pallas_call x1 -> x3, Pallas kernels: 4.24 us -> 8.02 us  [the longest x1 4.13 us: make_view(): pl.pallas_call(view_kernel, out_shape=(jax.ShapeDtypeStruct((whiten.shape...]
    ppermute x0 -> x2, waiting for transfers between devices: none -> 3.46 us  [the longest x1 1.74 us: on_device(): lax.ppermute(view, 'mod', partner)]
    all_to_all x2 -> x1, starting transfers between devices: 6.82 us -> 3.41 us  [swap(): return lax.all_to_all(x, axis, 0, 0, tiled=True, axis_index_groups=groups)]
    dot_general x1 -> x0, matrix products: 1.82 us -> none  [on_device(): lax.dot_general(panel_own, raw_grad, (((0,), (0,)), ((), ())), preferred_...]
    unnamed x4 -> x8, local copies, waits for them, and re-layouts: 0.71 us -> 2.13 us
  transfers between devices with their start and end apart: 2 -> 3, of which waited for: 2 -> 3; matrix products, arithmetic and copies ran while one was open for 0% -> 0% of each run, Pallas kernels for 0% -> 0%
where the time goes in v4:
time: 126 us; the launch traced here: 124 us
  blocking collectives  63.9 us (51%)
  Pallas kernels  40.2 us (32%)
  waiting for transfers between devices  10 us (8%)
  local copies, waits for them, and re-layouts  4.44 us (4%)
  starting transfers between devices  3.42 us (3%)
  other arithmetic  1.45 us (1%)
    all_to_all x3, blocking collectives, swap(): return lax.all_to_all(x, axis, 0, 0, tiled=True, axis_index_groups=groups)  63.9 us
    pallas_call x1, Pallas kernels, encode(): pl.pallas_call(conv_kernel, out_shape=jax.ShapeDtypeStruct((got.shape[0],...  18.6 us
    pallas_call x1, Pallas kernels, finish(): pl.pallas_call(tail_kernel, out_shape=(jax.ShapeDtypeStruct((share, width...  13.6 us
    all_to_all x1, waiting for transfers between devices, swap(): return lax.all_to_all(x, axis, 0, 0, tiled=True, axis_index_groups=groups)  6.56 us
    pallas_call x1, Pallas kernels, make_view(): pl.pallas_call(view_kernel, out_shape=(jax.ShapeDtypeStruct((whiten.shape...  4.13 us
    all_to_all x1, starting transfers between devices, swap(): return lax.all_to_all(x, axis, 0, 0, tiled=True, axis_index_groups=groups)  3.41 us
  transfers between devices with their start and end apart: 3, of which 3 were waited for; matrix products, arithmetic and copies ran while one was open for 0% of the time, Pallas kernels for 0%

profile of v4, /device:TPU:0, one launch (start us, length us, event | category | flops | bytes accessed | tf_op | source)
XLA Modules:
  0.0 124.0 jit_solution(10057518932662712989)
XLA Ops:
  0.6 0.7 convert_element_type.14
  1.4 0.1 convert_element_type.15
  1.5 0.1 convert_element_type.17
  1.6 2.1 %copy.10 = bf16[8,64,8,256]{3,1,2,0:T(8,128)(2,1)S(1)} copy(bf16[8,64,8,256]{3,2,1,0:T(8,128)(2,1)} %bitcast.20) | data formatting | bytes 4194304 | tf_op jit(solution)/shard_map/reshape;squeeze | solution.py:402
  3.7 0.1 fusion.1
  3.8 34.1 %all_to_all.20.got_ref = bf16[8,520,256]{2,1,0:T(8,128)(2,1)} all-to-all(bf16[8,520,256]{2,1,0:T(8,128)(2,1)S(1)} %fusion.1), channel_id=1, replica_groups=mesh['mod'=16,'sp'=8] {'sp'}, dimensions={0} | all-to-all | bytes 4259840 | tf_op jit(solution)/shard_map/all_to_all | solution.py:392
  38.0 18.6 %encode.1 = bf16[8,64,256]{2,1,0:T(8,128)(2,1)} custom-call(bf16[8,520,256]{2,1,0:T(8,128)(2,1)} %all_to_all.20.got_ref, bf16[256,256]{1,0:T(8,128)(2,1)} %bitcast.25, bf16[4096,256]{1,0:T(8,128)(2,1)} %bitcast.21), custom_call_target="tpu_custom_call" | custom-call | tf_op jit(solution)/shard_map/encode/pallas_call | solution.py:107
  56.5 3.4 %all-to-all-start.1 = ((bf16[8,64,256]{2,1,0:T(8,128)(2,1)}), bf16[8,64,256]{2,1,0:T(8,128)(2,1)S(1)}, u32[]{:S(2)}, u32[]{:S(2)}) async-start(bf16[8,64,256]{2,1,0:T(8,128)(2,1)} %encode.1), calls=%async_computation.1 | async-start | bytes 524288 | tf_op jit(solution)/shard_map/all_to_all | solution.py:392
  60.0 0.6 pad_add_fusion.place_ref
  60.5 6.6 %all-to-all-done.1 = bf16[8,64,256]{2,1,0:T(8,128)(2,1)S(1)} async-done(((bf16[8,64,256]{2,1,0:T(8,128)(2,1)}), bf16[8,64,256]{2,1,0:T(8,128)(2,1)S(1)}, u32[]{:S(2)}, u32[]{:S(2)}) %all-to-all-start.1) | async-done | bytes 262176 | tf_op jit(solution)/shard_map/all_to_all | solution.py:392
  67.1 0.0 copy-start.1
  67.1 0.7 copy-done.1
  67.8 4.1 %view.1 = (bf16[64,512]{1,0:T(8,128)(2,1)}, bf16[512,256]{1,0:T(8,128)(2,1)}, f32[512,128]{1,0:T(8,128)}) custom-call(s32[2]{0:T(128)} %pad_add_fusion.place_ref, bf16[512,256]{1,0:T(8,128)(2,1)} %bitcast.22, bf16[256,512]{1,0:T(8,128)(2,1)} %bitcast.23, bf16[512,256]{1,0:T(8,128)(2,1)} %bitcast.24, s32[1,512]{1,0:T(1,128)} %bitcast.27), custom_call_target="tpu_custom_call" | custom-call | tf_op jit(solution)/shard_map/view/pallas_call | solution.py:158
  71.9 0.0 collective-permute-start
  71.9 1.7 %collective-permute-done.other_ref = bf16[512,256]{1,0:T(8,128)(2,1)S(1)} collective-permute-done((bf16[512,256]{1,0:T(8,128)(2,1)}, bf16[512,256]{1,0:T(8,128)(2,1)S(1)}, u32[]{:S(2)}, u32[]{:S(2)}) %collective-permute-start) | collective-permute-done | bytes 262176 | tf_op jit(solution)/shard_map/ppermute | solution.py:417
  73.7 0.0 copy-start.3
  73.7 0.7 copy-done.3
  74.4 2.1 %pair.1 = bf16[8,96,256]{2,1,0:T(8,128)(2,1)} custom-call(s32[2]{0:T(128)} %pad_add_fusion.place_ref, bf16[512,256]{1,0:T(8,128)(2,1)} %get-tuple-element.9.view_ref, bf16[512,256]{1,0:T(8,128)(2,1)} %copy-done.3), custom_call_target="tpu_custom_call" | custom-call | tf_op jit(solution)/shard_map/pair/pallas_call | solution.py:192
  76.5 17.0 %all_to_all.21.in_ref = bf16[8,96,256]{2,1,0:T(8,128)(2,1)} all-to-all(bf16[8,96,256]{2,1,0:T(8,128)(2,1)} %pair.1), channel_id=1, replica_groups={{0,16,32,48,64,80,96,112},{8,24,40,56,72,88,104,120},{1,17,33,49,65,81,..., dimensions={0} | all-to-all | bytes 786432 | tf_op jit(solution)/shard_map/all_to_all | solution.py:392
  93.5 1.8 %sums.1 = bf16[8,96,256]{2,1,0:T(8,128)(2,1)} custom-call(bf16[8,96,256]{2,1,0:T(8,128)(2,1)} %all_to_all.21.in_ref), custom_call_target="tpu_custom_call" | custom-call | tf_op jit(solution)/shard_map/sums/pallas_call | solution.py:212
  95.3 12.7 %all_to_all.22.sums_ref = bf16[8,96,256]{2,1,0:T(8,128)(2,1)S(1)} all-to-all(bf16[8,96,256]{2,1,0:T(8,128)(2,1)} %sums.1), channel_id=1, replica_groups={{0,16,32,48,64,80,96,112},{8,24,40,56,72,88,104,120},{1,17,33,49,65,81,..., dimensions={0} | all-to-all | bytes 786432 | tf_op jit(solution)/shard_map/all_to_all | solution.py:392
  108.0 0.0 copy-start
  108.0 0.0 collective-permute-start.1
  108.0 1.7 %collective-permute-done.1.other_ref = bf16[8,96,256]{2,1,0:T(8,128)(2,1)S(1)} collective-permute-done((bf16[8,96,256]{2,1,0:T(8,128)(2,1)S(1)}, bf16[8,96,256]{2,1,0:T(8,128)(2,1)S(1)}, u32[]{:S(2)}, u32[]{:S(2)}) %collective-permute-start.1) | collective-permute-done | bytes 393248 | tf_op jit(solution)/shard_map/ppermute | solution.py:420
  109.7 0.0 copy-start.2
  109.7 0.0 copy-done
  109.7 0.7 copy-done.2
  110.4 13.6 %finish.1 = (f32[64,256]{1,0:T(8,128)}, bf16[64,256]{1,0:T(8,128)(2,1)}, f32[64,256]{1,0:T(8,128)}) custom-call(s32[2]{0:T(128)} %pad_add_fusion.place_ref, bf16[8,96,256]{2,1,0:T(8,128)(2,1)} %copy-done, bf16[8,96,256]{2,1,0:T(8,128)(2,1)} %copy-done.2, bf16[512,256]{1,0:T(8,128)(2,1)} %get-tuple-element.9.view_ref, ...), custom_call_target="tpu_custom_call" | custom-call | tf_op jit(solution)/shard_map/finish/pallas_call | solution.py:374
  (1 shorter events, 0.0 us)
Async XLA Ops:
  56.5 10.6 %all-to-all-start.1 = ((bf16[8,64,256]{2,1,0:T(8,128)(2,1)}), bf16[8,64,256]{2,1,0:T(8,128)(2,1)S(1)}, u32[]{:S(2)}, u32[]{:S(2)}) async-start(bf16[8,64,256]{2,1,0:T(8,128)(2,1)} %encode.1), calls=%async_computation.1 | async-start | bytes 524288 | tf_op jit(solution)/shard_map/all_to_all | solution.py:392
  67.1 0.7 copy-start.1
  71.9 1.7 %collective-permute-start = (bf16[512,256]{1,0:T(8,128)(2,1)}, bf16[512,256]{1,0:T(8,128)(2,1)S(1)}, u32[]{:S(2)}, u32[]{:S(2)}) collective-permute-start(bf16[512,256]{1,0:T(8,128)(2,1)} %get-tuple-element.9.view_ref), channel_id=1, source_target_pairs={{0,8},{8,0},{16,24},{24,16},{32,40},{40,32},{48,56},{56,48},{64,72... | collective-permute-start | bytes 786440 | tf_op jit(solution)/shard_map/ppermute | solution.py:417
  73.7 0.7 copy-start.3
  108.0 1.7 %copy-start = (bf16[8,96,256]{2,1,0:T(8,128)(2,1)}, bf16[8,96,256]{2,1,0:T(8,128)(2,1)S(1)}, u32[]{:S(2)}) copy-start(bf16[8,96,256]{2,1,0:T(8,128)(2,1)S(1)} %all_to_all.22.sums_ref) | copy-start | bytes 1179652
  108.0 1.7 %collective-permute-start.1 = (bf16[8,96,256]{2,1,0:T(8,128)(2,1)S(1)}, bf16[8,96,256]{2,1,0:T(8,128)(2,1)S(1)}, u32[]{:S(2)}, u32[]{:S(2)}) collective-permute-start(bf16[8,96,256]{2,1,0:T(8,128)(2,1)S(1)} %all_to_all.22.sums_ref), channel_id=1, source_target_pairs={{0,8},{8,0},{16,24},{24,16},{32,40},{40,32},{48,56},{56,48},{64,72... | collective-permute-start | bytes 1179656 | tf_op jit(solution)/shard_map/ppermute | solution.py:420
  109.7 0.7 copy-start.2

commit v5 on v4

--- a/solution.py
+++ b/solution.py
@@ -114,7 +114,7 @@
             pltpu.VMEM((512, 8 * CH), jnp.bfloat16),
             pltpu.VMEM((rows // 4 + 1, 2, share, 8 * CH), jnp.bfloat16),
         ],
-        compiler_params=pltpu.CompilerParams(vmem_limit_bytes=56 * 1024 * 1024),
+        compiler_params=pltpu.CompilerParams(vmem_limit_bytes=24 * 1024 * 1024),
         name="encode",
     )(got, w1, w2)
 
@@ -164,6 +164,7 @@
         ),
         in_specs=[pl.BlockSpec(memory_space=pltpu.SMEM)] + [vmem] * 4,
         out_specs=(vmem,) * 3,
+        compiler_params=pltpu.CompilerParams(vmem_limit_bytes=12 * 1024 * 1024),
         name="view",
     )(place, pooled, project, whiten, scene)
 
@@ -194,6 +195,7 @@
         out_shape=jax.ShapeDtypeStruct((chips, 3 * block, CH), jnp.bfloat16),
         in_specs=[pl.BlockSpec(memory_space=pltpu.SMEM), vmem, vmem],
         out_specs=vmem,
+        compiler_params=pltpu.CompilerParams(vmem_limit_bytes=8 * 1024 * 1024),
         name="pair",
     )(place, view, other)
 
@@ -214,6 +216,7 @@
         out_shape=jax.ShapeDtypeStruct(x.shape, x.dtype),
         in_specs=[vmem],
         out_specs=vmem,
+        compiler_params=pltpu.CompilerParams(vmem_limit_bytes=6 * 1024 * 1024),
         name="sums",
     )(x)
 
@@ -384,6 +387,7 @@
             pltpu.VMEM((width, 2 * width), jnp.float32),
             pltpu.VMEM((samples, width), jnp.float32),
         ],
+        compiler_params=pltpu.CompilerParams(vmem_limit_bytes=12 * 1024 * 1024),
         name="finish",
     )(place, sums, other, view, scale, columns)
 

time: 126 us -> 115 us (0.913)
  Pallas kernels: 40.2 us -> 32.8 us
  local copies, waits for them, and re-layouts: 4.44 us -> 2.34 us
    pallas_call x1, Pallas kernels: 18.6 us -> 16.3 us  [encode(): pl.pallas_call(conv_kernel, out_shape=jax.ShapeDtypeStruct((got.shape[0],...]
    unnamed x8 -> x10, local copies, waits for them, and re-layouts: 2.13 us -> 0.03 us
    pallas_call x1, Pallas kernels: 1.79 us -> 0.06 us  [sum_spread(): pl.pallas_call(sum_kernel, out_shape=jax.ShapeDtypeStruct(x.shape, x.dtyp...]
    pallas_call x1, Pallas kernels: 4.13 us -> 2.75 us  [make_view(): pl.pallas_call(view_kernel, out_shape=(jax.ShapeDtypeStruct((whiten.shape...]
where the time goes in v5:
time: 115 us; the launch traced here: 114 us
  blocking collectives  63.1 us (55%)
  Pallas kernels  32.8 us (29%)
  waiting for transfers between devices  10.3 us (9%)
  starting transfers between devices  3.5 us (3%)
  local copies, waits for them, and re-layouts  2.34 us (2%)
    all_to_all x3, blocking collectives, swap(): return lax.all_to_all(x, axis, 0, 0, tiled=True, axis_index_groups=groups)  63.1 us
    pallas_call x1, Pallas kernels, encode(): pl.pallas_call(conv_kernel, out_shape=jax.ShapeDtypeStruct((got.shape[0],...  16.3 us
    pallas_call x1, Pallas kernels, finish(): pl.pallas_call(tail_kernel, out_shape=(jax.ShapeDtypeStruct((share, width...  12.9 us
    all_to_all x1, waiting for transfers between devices, swap(): return lax.all_to_all(x, axis, 0, 0, tiled=True, axis_index_groups=groups)  7.07 us
    all_to_all x1, starting transfers between devices, swap(): return lax.all_to_all(x, axis, 0, 0, tiled=True, axis_index_groups=groups)  3.41 us
    pallas_call x1, Pallas kernels, make_view(): pl.pallas_call(view_kernel, out_shape=(jax.ShapeDtypeStruct((whiten.shape...  2.75 us
  transfers between devices with their start and end apart: 3, of which 3 were waited for; matrix products, arithmetic and copies ran while one was open for 0% of the time, Pallas kernels for 0%

profile of v5, /device:TPU:0, one launch (start us, length us, event | category | flops | bytes accessed | tf_op | source)
XLA Modules:
  0.0 113.7 jit_solution(10085906486542214312)
XLA Ops:
  0.6 0.7 convert_element_type.14
  1.4 0.1 convert_element_type.15
  1.5 0.1 convert_element_type.17
  1.6 2.1 %copy.10 = bf16[8,64,8,256]{3,1,2,0:T(8,128)(2,1)S(1)} copy(bf16[8,64,8,256]{3,2,1,0:T(8,128)(2,1)} %bitcast.26) | data formatting | bytes 4194304 | tf_op jit(solution)/shard_map/reshape;squeeze | solution.py:406
  3.7 0.1 fusion.1
  3.8 0.0 copy-start
  3.8 0.0 copy-start.3
  3.9 34.2 %all_to_all.20.got_ref = bf16[8,520,256]{2,1,0:T(8,128)(2,1)S(1)} all-to-all(bf16[8,520,256]{2,1,0:T(8,128)(2,1)S(1)} %fusion.1), channel_id=1, replica_groups=mesh['mod'=16,'sp'=8] {'sp'}, dimensions={0} | all-to-all | bytes 4259840 | tf_op jit(solution)/shard_map/all_to_all | solution.py:396
  38.0 0.0 copy-done
  38.0 0.0 copy-done.3
  38.0 0.0 copy-start.1
  38.0 0.0 copy-start.2
  38.0 0.0 copy-start.4
  38.0 16.3 %encode.1 = bf16[8,64,256]{2,1,0:T(8,128)(2,1)} custom-call(bf16[8,520,256]{2,1,0:T(8,128)(2,1)S(1)} %all_to_all.20.got_ref, bf16[256,256]{1,0:T(8,128)(2,1)S(1)} %bitcast.23, bf16[4096,256]{1,0:T(8,128)(2,1)S(1)} %bitcast.19), custom_call_target="tpu_custom_call" | custom-call | tf_op jit(solution)/shard_map/encode/pallas_call | solution.py:107
  54.3 3.4 %all-to-all-start.1 = ((bf16[8,64,256]{2,1,0:T(8,128)(2,1)}), bf16[8,64,256]{2,1,0:T(8,128)(2,1)S(1)}, u32[]{:S(2)}, u32[]{:S(2)}) async-start(bf16[8,64,256]{2,1,0:T(8,128)(2,1)} %encode.1), calls=%async_computation.1 | async-start | bytes 524288 | tf_op jit(solution)/shard_map/all_to_all | solution.py:396
  57.7 0.1 pad_add_fusion.place_ref
  57.8 7.1 %all-to-all-done.1 = bf16[8,64,256]{2,1,0:T(8,128)(2,1)S(1)} async-done(((bf16[8,64,256]{2,1,0:T(8,128)(2,1)}), bf16[8,64,256]{2,1,0:T(8,128)(2,1)S(1)}, u32[]{:S(2)}, u32[]{:S(2)}) %all-to-all-start.1) | async-done | bytes 262176 | tf_op jit(solution)/shard_map/all_to_all | solution.py:396
  64.9 0.0 copy-done.1
  64.9 0.0 copy-done.2
  64.9 0.0 copy-done.4
  64.9 2.8 %view.1 = (bf16[64,512]{1,0:T(8,128)(2,1)S(1)}, bf16[512,256]{1,0:T(8,128)(2,1)S(1)}, f32[512,128]{1,0:T(8,128)S(1)}) custom-call(s32[2]{0:T(128)S(1)} %pad_add_fusion.place_ref, bf16[512,256]{1,0:T(8,128)(2,1)S(1)} %bitcast.20, bf16[256,512]{1,0:T(8,128)(2,1)S(1)} %bitcast.21, bf16[512,256]{1,0:T(8,128)(2,1)S(1)} %bitcast.22, s32[1,512]{1,0:T(1,128)S(1)} %bitcast.24), custom_call_target="tpu_custom_call" | custom-call | tf_op jit(solution)/shard_map/view/pallas_call | solution.py:158
  67.6 0.1 collective-permute-start
  67.7 1.5 %collective-permute-done.other_ref = bf16[512,256]{1,0:T(8,128)(2,1)S(1)} collective-permute-done((bf16[512,256]{1,0:T(8,128)(2,1)S(1)}, bf16[512,256]{1,0:T(8,128)(2,1)S(1)}, u32[]{:S(2)}, u32[]{:S(2)}) %collective-permute-start) | collective-permute-done | bytes 262176 | tf_op jit(solution)/shard_map/ppermute | solution.py:421
  69.3 0.9 pair.1
  70.1 16.7 %all_to_all.21.in_ref = bf16[8,96,256]{2,1,0:T(8,128)(2,1)S(1)} all-to-all(bf16[8,96,256]{2,1,0:T(8,128)(2,1)S(1)} %pair.1), channel_id=1, replica_groups={{0,16,32,48,64,80,96,112},{8,24,40,56,72,88,104,120},{1,17,33,49,65,81,..., dimensions={0} | all-to-all | bytes 786432 | tf_op jit(solution)/shard_map/all_to_all | solution.py:396
  86.9 0.1 sums.1
  86.9 12.2 %all_to_all.22.sums_ref = bf16[8,96,256]{2,1,0:T(8,128)(2,1)S(1)} all-to-all(bf16[8,96,256]{2,1,0:T(8,128)(2,1)S(1)} %sums.1), channel_id=1, replica_groups={{0,16,32,48,64,80,96,112},{8,24,40,56,72,88,104,120},{1,17,33,49,65,81,..., dimensions={0} | all-to-all | bytes 786432 | tf_op jit(solution)/shard_map/all_to_all | solution.py:396
  99.1 0.0 collective-permute-start.1
  99.1 1.7 %collective-permute-done.1.other_ref = bf16[8,96,256]{2,1,0:T(8,128)(2,1)S(1)} collective-permute-done((bf16[8,96,256]{2,1,0:T(8,128)(2,1)S(1)}, bf16[8,96,256]{2,1,0:T(8,128)(2,1)S(1)}, u32[]{:S(2)}, u32[]{:S(2)}) %collective-permute-start.1) | collective-permute-done | bytes 393248 | tf_op jit(solution)/shard_map/ppermute | solution.py:424
  100.8 12.9 %finish.1 = (f32[64,256]{1,0:T(8,128)}, bf16[64,256]{1,0:T(8,128)(2,1)}, f32[64,256]{1,0:T(8,128)}) custom-call(s32[2]{0:T(128)S(1)} %pad_add_fusion.place_ref, bf16[8,96,256]{2,1,0:T(8,128)(2,1)S(1)} %all_to_all.22.sums_ref, bf16[8,96,256]{2,1,0:T(8,128)(2,1)S(1)} %collective-permute-done.1.other_ref, bf16[512,256]{1,0:T(8,128)(2,1)S(1)} %get-tuple-element.9.view_ref, ...), custom_call_target="tpu_custom_call" | custom-call | tf_op jit(solution)/shard_map/finish/pallas_call | solution.py:377
  (1 shorter events, 0.0 us)
Async XLA Ops:
  3.8 34.2 %copy-start = (bf16[1,4096,256]{2,1,0:T(8,128)(2,1)S(1)}, bf16[1,4096,256]{2,1,0:T(8,128)(2,1)}, u32[]{:S(2)}) copy-start(bf16[1,4096,256]{2,1,0:T(8,128)(2,1)} %param.9) | copy-start | bytes 6291460
  3.8 34.2 %copy-start.3 = (bf16[1,256,256]{2,1,0:T(8,128)(2,1)S(1)}, bf16[1,256,256]{2,1,0:T(8,128)(2,1)}, u32[]{:S(2)}) copy-start(bf16[1,256,256]{2,1,0:T(8,128)(2,1)} %param.8) | copy-start | bytes 393220
  38.0 26.9 %copy-start.1 = (bf16[1,256,512]{2,1,0:T(8,128)(2,1)S(1)}, bf16[1,256,512]{2,1,0:T(8,128)(2,1)}, u32[]{:S(2)}) copy-start(bf16[1,256,512]{2,1,0:T(8,128)(2,1)} %param.10) | copy-start | bytes 786436
  38.0 26.9 %copy-start.2 = (bf16[1,512,256]{2,1,0:T(8,128)(2,1)S(1)}, bf16[1,512,256]{2,1,0:T(8,128)(2,1)}, u32[]{:S(2)}) copy-start(bf16[1,512,256]{2,1,0:T(8,128)(2,1)} %param.11) | copy-start | bytes 786436
  38.0 26.8 %copy-start.4 = (s32[512]{0:T(512)S(1)}, s32[512]{0:T(512)}, u32[]{:S(2)}) copy-start(s32[512]{0:T(512)} %param.13) | copy-start | bytes 6148
  54.3 10.6 %all-to-all-start.1 = ((bf16[8,64,256]{2,1,0:T(8,128)(2,1)}), bf16[8,64,256]{2,1,0:T(8,128)(2,1)S(1)}, u32[]{:S(2)}, u32[]{:S(2)}) async-start(bf16[8,64,256]{2,1,0:T(8,128)(2,1)} %encode.1), calls=%async_computation.1 | async-start | bytes 524288 | tf_op jit(solution)/shard_map/all_to_all | solution.py:396
  67.6 1.6 %collective-permute-start = (bf16[512,256]{1,0:T(8,128)(2,1)S(1)}, bf16[512,256]{1,0:T(8,128)(2,1)S(1)}, u32[]{:S(2)}, u32[]{:S(2)}) collective-permute-start(bf16[512,256]{1,0:T(8,128)(2,1)S(1)} %get-tuple-element.9.view_ref), channel_id=1, source_target_pairs={{0,8},{8,0},{16,24},{24,16},{32,40},{40,32},{48,56},{56,48},{64,72... | collective-permute-start | bytes 786440 | tf_op jit(solution)/shard_map/ppermute | solution.py:421
  99.1 1.7 %collective-permute-start.1 = (bf16[8,96,256]{2,1,0:T(8,128)(2,1)S(1)}, bf16[8,96,256]{2,1,0:T(8,128)(2,1)S(1)}, u32[]{:S(2)}, u32[]{:S(2)}) collective-permute-start(bf16[8,96,256]{2,1,0:T(8,128)(2,1)S(1)} %all_to_all.22.sums_ref), channel_id=1, source_target_pairs={{0,8},{8,0},{16,24},{24,16},{32,40},{40,32},{48,56},{56,48},{64,72... | collective-permute-start | bytes 1179656 | tf_op jit(solution)/shard_map/ppermute | solution.py:424

commit v6 on v5

--- a/solution.py
+++ b/solution.py
@@ -43,13 +43,15 @@
     first_ref[0, 0] = blank
     first_ref[total_rows // 4, 1] = blank
 
+    step = 16
+
     def first_rows(group, carry):
         for start, columns in groups:
             left = jnp.concatenate(
                 [
                     padded_ref[
-                        pl.ds(group * 8 + tap // 2, 8), tap % 2, :, start : start + 128
-                    ].reshape(8 * share, 128)
+                        pl.ds(group * step + tap // 2, step), tap % 2, :, start : start + 128
+                    ].reshape(step * share, 128)
                     for tap in range(4)
                 ],
                 axis=1,
@@ -57,26 +59,30 @@
             lanes = slice(columns[0] * CH, (columns[-1] + 1) * CH)
             total = jnp.dot(left, band_ref[:, lanes], preferred_element_type=jnp.float32)
             total = jnp.maximum(total, 0.0).astype(jnp.bfloat16)
-            for row in range(8):
-                first_ref[group * 4 + (row + 1) // 2, (row + 1) % 2, :, lanes] = total[
+            for row in range(step):
+                first_ref[group * (step // 2) + (row + 1) // 2, (row + 1) % 2, :, lanes] = total[
                     row * share : (row + 1) * share
                 ]
         return carry
 
-    lax.fori_loop(0, total_rows // 16, first_rows, 0)
-
-    span = 8 * share
+    lax.fori_loop(0, total_rows // 2 // step, first_rows, 0)
+
+    chunk = total_rows // 4
+    span = chunk * share
     spot = lax.broadcasted_iota(jnp.int32, (share, span), 1) % share
     mine = spot == lax.broadcasted_iota(jnp.int32, (share, span), 0)
     pooled = jnp.zeros((share, CH), jnp.float32)
-    for group in range(total_rows // 32):
+    for group in range(total_rows // 4 // chunk):
         for column in range(4):
             low, high = (max(2 * column - 1, 0), min(2 * column + 3, 8))
             skip = low - (2 * column - 1)
             total = None
             for tap in range(4):
                 left = first_ref[
-                    group * 8 + tap // 2 : group * 8 + tap // 2 + 8, tap % 2, :, low * CH : high * CH
+                    group * chunk + tap // 2 : group * chunk + tap // 2 + chunk,
+                    tap % 2,
+                    :,
+                    low * CH : high * CH,
                 ]
                 part = jnp.dot(
                     left.reshape(span, (high - low) * CH),
@@ -88,8 +94,8 @@
             row = rows * share + column
             valid = jnp.concatenate(
                 [
-                    got_ref[group * 4 + source, row : row + 1, : 2 * share].astype(jnp.float32)
-                    for source in range(4)
+                    got_ref[group * chunk // 2 + source, row : row + 1, : 2 * share].astype(jnp.float32)
+                    for source in range(chunk // 2)
                 ],
                 axis=1,
             )
@@ -119,24 +125,30 @@
     )(got, w1, w2)
 
 
+def chosen_sums(onehot, values, over):
+    total = None
+    for _ in range(3):
+        part = values.astype(jnp.bfloat16)
+        values = values - part.astype(jnp.float32)
+        product = lax.dot_general(
+            onehot, part, (((over,), (0,)), ((), ())), preferred_element_type=jnp.float32
+        )
+        total = product if total is None else total + product
+    return total
+
+
 def view_kernel(
     place_ref, pooled_ref, project_ref, whiten_ref, scene_ref, columns_ref, view_ref, scale_ref
 ):
     samples = pooled_ref.shape[0]
-    exact = lax.Precision.HIGHEST
     feat = jnp.dot(pooled_ref[...], project_ref[...], preferred_element_type=jnp.float32)
     scene = lax.broadcasted_iota(jnp.int32, (SCENES, samples), 0)
     onehot = jnp.where(scene == scene_ref[...], 1.0, 0.0)
     counts = jnp.sum(onehot, axis=1, keepdims=True)
-    sums = jnp.dot(onehot, feat, precision=exact, preferred_element_type=jnp.float32)
+    half_onehot = onehot.astype(jnp.bfloat16)
+    sums = chosen_sums(half_onehot, feat, 1)
     means = sums / jnp.maximum(counts, 1.0)
-    own = lax.dot_general(
-        onehot,
-        means,
-        (((0,), (0,)), ((), ())),
-        precision=exact,
-        preferred_element_type=jnp.float32,
-    )
+    own = chosen_sums(half_onehot, means, 0)
     panel = (feat - own).astype(jnp.bfloat16)
     raw = jnp.dot(panel, whiten_ref[...], preferred_element_type=jnp.float32)
     scale = lax.rsqrt(jnp.mean(raw * raw, axis=-1, keepdims=True) + 1e-05)

time: 115 us -> 114 us (level)
  Pallas kernels: 32.8 us -> 31.3 us
where the time goes in v6:
time: 114 us; the launch traced here: 112 us
  blocking collectives  63.1 us (55%)
  Pallas kernels  31.3 us (27%)
  waiting for transfers between devices  10.3 us (9%)
  starting transfers between devices  3.5 us (3%)
  local copies, waits for them, and re-layouts  2.34 us (2%)
    all_to_all x3, blocking collectives, swap(): return lax.all_to_all(x, axis, 0, 0, tiled=True, axis_index_groups=groups)  63.1 us
    pallas_call x1, Pallas kernels, encode(): pl.pallas_call(conv_kernel, out_shape=jax.ShapeDtypeStruct((got.shape[0],...  15.4 us
    pallas_call x1, Pallas kernels, finish(): pl.pallas_call(tail_kernel, out_shape=(jax.ShapeDtypeStruct((share, width...  12.9 us
    all_to_all x1, waiting for transfers between devices, swap(): return lax.all_to_all(x, axis, 0, 0, tiled=True, axis_index_groups=groups)  7.07 us
    all_to_all x1, starting transfers between devices, swap(): return lax.all_to_all(x, axis, 0, 0, tiled=True, axis_index_groups=groups)  3.41 us
  transfers between devices with their start and end apart: 3, of which 3 were waited for; matrix products, arithmetic and copies ran while one was open for 0% of the time, Pallas kernels for 0%

profile of v6, /device:TPU:0, one launch (start us, length us, event | category | flops | bytes accessed | tf_op | source)
XLA Modules:
  0.0 112.2 jit_solution(12509447495384600425)
XLA Ops:
  0.6 0.7 convert_element_type.14
  1.4 0.1 convert_element_type.15
  1.5 0.1 convert_element_type.17
  1.6 2.1 %copy.10 = bf16[8,64,8,256]{3,1,2,0:T(8,128)(2,1)S(1)} copy(bf16[8,64,8,256]{3,2,1,0:T(8,128)(2,1)} %bitcast.26) | data formatting | bytes 4194304 | tf_op jit(solution)/shard_map/reshape;squeeze | solution.py:418
  3.7 0.1 fusion.1
  3.8 0.0 copy-start
  3.8 0.0 copy-start.3
  3.9 34.2 %all_to_all.20.got_ref = bf16[8,520,256]{2,1,0:T(8,128)(2,1)S(1)} all-to-all(bf16[8,520,256]{2,1,0:T(8,128)(2,1)S(1)} %fusion.1), channel_id=1, replica_groups=mesh['mod'=16,'sp'=8] {'sp'}, dimensions={0} | all-to-all | bytes 4259840 | tf_op jit(solution)/shard_map/all_to_all | solution.py:408
  38.0 0.0 copy-done
  38.0 0.0 copy-done.3
  38.0 0.0 copy-start.1
  38.0 0.0 copy-start.2
  38.0 0.0 copy-start.4
  38.0 15.4 %encode.1 = bf16[8,64,256]{2,1,0:T(8,128)(2,1)} custom-call(bf16[8,520,256]{2,1,0:T(8,128)(2,1)S(1)} %all_to_all.20.got_ref, bf16[256,256]{1,0:T(8,128)(2,1)S(1)} %bitcast.23, bf16[4096,256]{1,0:T(8,128)(2,1)S(1)} %bitcast.19), custom_call_target="tpu_custom_call" | custom-call | tf_op jit(solution)/shard_map/encode/pallas_call | solution.py:113
  53.4 3.4 %all-to-all-start.1 = ((bf16[8,64,256]{2,1,0:T(8,128)(2,1)}), bf16[8,64,256]{2,1,0:T(8,128)(2,1)S(1)}, u32[]{:S(2)}, u32[]{:S(2)}) async-start(bf16[8,64,256]{2,1,0:T(8,128)(2,1)} %encode.1), calls=%async_computation.1 | async-start | bytes 524288 | tf_op jit(solution)/shard_map/all_to_all | solution.py:408
  56.9 0.1 pad_add_fusion.place_ref
  57.0 7.1 %all-to-all-done.1 = bf16[8,64,256]{2,1,0:T(8,128)(2,1)S(1)} async-done(((bf16[8,64,256]{2,1,0:T(8,128)(2,1)}), bf16[8,64,256]{2,1,0:T(8,128)(2,1)S(1)}, u32[]{:S(2)}, u32[]{:S(2)}) %all-to-all-start.1) | async-done | bytes 262176 | tf_op jit(solution)/shard_map/all_to_all | solution.py:408
  64.0 0.0 copy-done.1
  64.0 0.0 copy-done.2
  64.0 0.0 copy-done.4
  64.0 2.1 %view.1 = (bf16[64,512]{1,0:T(8,128)(2,1)S(1)}, bf16[512,256]{1,0:T(8,128)(2,1)S(1)}, f32[512,128]{1,0:T(8,128)S(1)}) custom-call(s32[2]{0:T(128)S(1)} %pad_add_fusion.place_ref, bf16[512,256]{1,0:T(8,128)(2,1)S(1)} %bitcast.20, bf16[256,512]{1,0:T(8,128)(2,1)S(1)} %bitcast.21, bf16[512,256]{1,0:T(8,128)(2,1)S(1)} %bitcast.22, s32[1,512]{1,0:T(1,128)S(1)} %bitcast.24), custom_call_target="tpu_custom_call" | custom-call | tf_op jit(solution)/shard_map/view/pallas_call | solution.py:170
  66.2 0.1 collective-permute-start
  66.2 1.5 %collective-permute-done.other_ref = bf16[512,256]{1,0:T(8,128)(2,1)S(1)} collective-permute-done((bf16[512,256]{1,0:T(8,128)(2,1)S(1)}, bf16[512,256]{1,0:T(8,128)(2,1)S(1)}, u32[]{:S(2)}, u32[]{:S(2)}) %collective-permute-start) | collective-permute-done | bytes 262176 | tf_op jit(solution)/shard_map/ppermute | solution.py:433
  67.8 0.9 pair.1
  68.7 16.7 %all_to_all.21.in_ref = bf16[8,96,256]{2,1,0:T(8,128)(2,1)S(1)} all-to-all(bf16[8,96,256]{2,1,0:T(8,128)(2,1)S(1)} %pair.1), channel_id=1, replica_groups={{0,16,32,48,64,80,96,112},{8,24,40,56,72,88,104,120},{1,17,33,49,65,81,..., dimensions={0} | all-to-all | bytes 786432 | tf_op jit(solution)/shard_map/all_to_all | solution.py:408
  85.4 0.1 sums.1
  85.5 12.2 %all_to_all.22.sums_ref = bf16[8,96,256]{2,1,0:T(8,128)(2,1)S(1)} all-to-all(bf16[8,96,256]{2,1,0:T(8,128)(2,1)S(1)} %sums.1), channel_id=1, replica_groups={{0,16,32,48,64,80,96,112},{8,24,40,56,72,88,104,120},{1,17,33,49,65,81,..., dimensions={0} | all-to-all | bytes 786432 | tf_op jit(solution)/shard_map/all_to_all | solution.py:408
  97.6 0.0 collective-permute-start.1
  97.6 1.7 %collective-permute-done.1.other_ref = bf16[8,96,256]{2,1,0:T(8,128)(2,1)S(1)} collective-permute-done((bf16[8,96,256]{2,1,0:T(8,128)(2,1)S(1)}, bf16[8,96,256]{2,1,0:T(8,128)(2,1)S(1)}, u32[]{:S(2)}, u32[]{:S(2)}) %collective-permute-start.1) | collective-permute-done | bytes 393248 | tf_op jit(solution)/shard_map/ppermute | solution.py:436
  99.3 12.9 %finish.1 = (f32[64,256]{1,0:T(8,128)}, bf16[64,256]{1,0:T(8,128)(2,1)}, f32[64,256]{1,0:T(8,128)}) custom-call(s32[2]{0:T(128)S(1)} %pad_add_fusion.place_ref, bf16[8,96,256]{2,1,0:T(8,128)(2,1)S(1)} %all_to_all.22.sums_ref, bf16[8,96,256]{2,1,0:T(8,128)(2,1)S(1)} %collective-permute-done.1.other_ref, bf16[512,256]{1,0:T(8,128)(2,1)S(1)} %get-tuple-element.9.view_ref, ...), custom_call_target="tpu_custom_call" | custom-call | tf_op jit(solution)/shard_map/finish/pallas_call | solution.py:389
  (1 shorter events, 0.0 us)
Async XLA Ops:
  3.8 34.2 %copy-start = (bf16[1,4096,256]{2,1,0:T(8,128)(2,1)S(1)}, bf16[1,4096,256]{2,1,0:T(8,128)(2,1)}, u32[]{:S(2)}) copy-start(bf16[1,4096,256]{2,1,0:T(8,128)(2,1)} %param.9) | copy-start | bytes 6291460
  3.8 34.2 %copy-start.3 = (bf16[1,256,256]{2,1,0:T(8,128)(2,1)S(1)}, bf16[1,256,256]{2,1,0:T(8,128)(2,1)}, u32[]{:S(2)}) copy-start(bf16[1,256,256]{2,1,0:T(8,128)(2,1)} %param.8) | copy-start | bytes 393220
  38.0 26.0 %copy-start.1 = (bf16[1,256,512]{2,1,0:T(8,128)(2,1)S(1)}, bf16[1,256,512]{2,1,0:T(8,128)(2,1)}, u32[]{:S(2)}) copy-start(bf16[1,256,512]{2,1,0:T(8,128)(2,1)} %param.10) | copy-start | bytes 786436
  38.0 26.0 %copy-start.2 = (bf16[1,512,256]{2,1,0:T(8,128)(2,1)S(1)}, bf16[1,512,256]{2,1,0:T(8,128)(2,1)}, u32[]{:S(2)}) copy-start(bf16[1,512,256]{2,1,0:T(8,128)(2,1)} %param.11) | copy-start | bytes 786436
  38.0 26.0 %copy-start.4 = (s32[512]{0:T(512)S(1)}, s32[512]{0:T(512)}, u32[]{:S(2)}) copy-start(s32[512]{0:T(512)} %param.13) | copy-start | bytes 6148
  53.4 10.6 %all-to-all-start.1 = ((bf16[8,64,256]{2,1,0:T(8,128)(2,1)}), bf16[8,64,256]{2,1,0:T(8,128)(2,1)S(1)}, u32[]{:S(2)}, u32[]{:S(2)}) async-start(bf16[8,64,256]{2,1,0:T(8,128)(2,1)} %encode.1), calls=%async_computation.1 | async-start | bytes 524288 | tf_op jit(solution)/shard_map/all_to_all | solution.py:408
  66.2 1.6 %collective-permute-start = (bf16[512,256]{1,0:T(8,128)(2,1)S(1)}, bf16[512,256]{1,0:T(8,128)(2,1)S(1)}, u32[]{:S(2)}, u32[]{:S(2)}) collective-permute-start(bf16[512,256]{1,0:T(8,128)(2,1)S(1)} %get-tuple-element.9.view_ref), channel_id=1, source_target_pairs={{0,8},{8,0},{16,24},{24,16},{32,40},{40,32},{48,56},{56,48},{64,72... | collective-permute-start | bytes 786440 | tf_op jit(solution)/shard_map/ppermute | solution.py:433
  97.6 1.7 %collective-permute-start.1 = (bf16[8,96,256]{2,1,0:T(8,128)(2,1)S(1)}, bf16[8,96,256]{2,1,0:T(8,128)(2,1)S(1)}, u32[]{:S(2)}, u32[]{:S(2)}) collective-permute-start(bf16[8,96,256]{2,1,0:T(8,128)(2,1)S(1)} %all_to_all.22.sums_ref), channel_id=1, source_target_pairs={{0,8},{8,0},{16,24},{24,16},{32,40},{40,32},{48,56},{56,48},{64,72... | collective-permute-start | bytes 1179656 | tf_op jit(solution)/shard_map/ppermute | solution.py:436

commit v7 on v6

--- a/solution.py
+++ b/solution.py
@@ -73,34 +73,38 @@
     mine = spot == lax.broadcasted_iota(jnp.int32, (share, span), 0)
     pooled = jnp.zeros((share, CH), jnp.float32)
     for group in range(total_rows // 4 // chunk):
-        for column in range(4):
-            low, high = (max(2 * column - 1, 0), min(2 * column + 3, 8))
-            skip = low - (2 * column - 1)
-            total = None
+        for columns in ((0, 3), (1, 2)):
+            totals = {}
             for tap in range(4):
-                left = first_ref[
-                    group * chunk + tap // 2 : group * chunk + tap // 2 + chunk,
-                    tap % 2,
-                    :,
-                    low * CH : high * CH,
-                ]
-                part = jnp.dot(
-                    left.reshape(span, (high - low) * CH),
-                    w2_ref[(tap * 4 + skip) * CH : (tap * 4 + skip + high - low) * CH, :],
-                    preferred_element_type=jnp.float32,
+                for column in columns:
+                    low, high = (max(2 * column - 1, 0), min(2 * column + 3, 8))
+                    skip = low - (2 * column - 1)
+                    left = first_ref[
+                        group * chunk + tap // 2 : group * chunk + tap // 2 + chunk,
+                        tap % 2,
+                        :,
+                        low * CH : high * CH,
+                    ]
+                    part = jnp.dot(
+                        left.reshape(span, (high - low) * CH),
+                        w2_ref[(tap * 4 + skip) * CH : (tap * 4 + skip + high - low) * CH, :],
+                        preferred_element_type=jnp.float32,
+                    )
+                    totals[column] = totals[column] + part if tap else part
+            for column in columns:
+                pixel = jnp.maximum(totals[column], 0.0).astype(jnp.bfloat16)
+                row = rows * share + column
+                valid = jnp.concatenate(
+                    [
+                        got_ref[
+                            group * chunk // 2 + source, row : row + 1, : 2 * share
+                        ].astype(jnp.float32)
+                        for source in range(chunk // 2)
+                    ],
+                    axis=1,
                 )
-                total = part if total is None else total + part
-            pixel = jnp.maximum(total, 0.0).astype(jnp.bfloat16)
-            row = rows * share + column
-            valid = jnp.concatenate(
-                [
-                    got_ref[group * chunk // 2 + source, row : row + 1, : 2 * share].astype(jnp.float32)
-                    for source in range(chunk // 2)
-                ],
-                axis=1,
-            )
-            chosen = jnp.where(mine, valid, 0.0).astype(jnp.bfloat16)
-            pooled = pooled + jnp.dot(chosen, pixel, preferred_element_type=jnp.float32)
+                chosen = jnp.where(mine, valid, 0.0).astype(jnp.bfloat16)
+                pooled = pooled + jnp.dot(chosen, pixel, preferred_element_type=jnp.float32)
     cells = total_rows // 4 * 4
     pooled = (pooled / cells).astype(jnp.bfloat16)
     for source in range(sources):
@@ -125,13 +129,13 @@
     )(got, w1, w2)
 
 
-def chosen_sums(onehot, values, over):
+def chosen_sums(left, values, over, other=0):
     total = None
     for _ in range(3):
         part = values.astype(jnp.bfloat16)
         values = values - part.astype(jnp.float32)
         product = lax.dot_general(
-            onehot, part, (((over,), (0,)), ((), ())), preferred_element_type=jnp.float32
+            left, part, (((over,), (other,)), ((), ())), preferred_element_type=jnp.float32
         )
         total = product if total is None else total + product
     return total
@@ -304,7 +308,7 @@
                     rows[h, t] = rows[h, t] - weight * spreads[j, t]
 
 
-def solve(work_ref):
+def solve(work_ref, beside):
     size = work_ref.shape[0]
     for top in range(0, size, BLOCK):
         factor_block(work_ref, top)
@@ -318,6 +322,8 @@
                 precision=lax.Precision.HIGHEST,
                 preferred_element_type=jnp.float32,
             )
+            if beside:
+                beside.pop(0)()
             work_ref[low:, start:] = work_ref[low:, start:] - change[low - start :]
 
 
@@ -348,7 +354,7 @@
             [jnp.where(core == 0, mine, other), jnp.where(core == 0, other, mine)], axis=0
         )
 
-    total = whole(0)
+    total, left, right = (whole(0), whole(1), whole(2))
     mean = total * (1.0 / MODS)
     gram = lax.dot_general(
         mean, mean, (((0,), (0,)), ((), ())), preferred_element_type=jnp.float32
@@ -357,16 +363,17 @@
     eye = lax.broadcasted_iota(jnp.int32, shape, 0) == lax.broadcasted_iota(jnp.int32, shape, 1)
     work_ref[:, :width] = gram / samples + jnp.where(eye, 0.001, 0.0)
     work_ref[:, width:] = jnp.where(eye, 1.0, 0.0)
-    solve(work_ref)
-    target = lax.dot_general(
-        mean.astype(jnp.float32),
-        work_ref[:, width:],
-        (((1,), (1,)), ((), ())),
-        precision=lax.Precision.HIGHEST,
-        preferred_element_type=jnp.float32,
-    )
-    coupling = jnp.dot(whole(1), view_ref[:width, :], preferred_element_type=jnp.float32)
-    coupling = coupling + jnp.dot(whole(2), view_ref[width:, :], preferred_element_type=jnp.float32)
+
+    def couple(low):
+        rows = slice(low, low + half)
+        part = jnp.dot(left[rows], view_ref[:width, :], preferred_element_type=jnp.float32)
+        full_ref[rows, :] = part + jnp.dot(
+            right[rows], view_ref[width:, :], preferred_element_type=jnp.float32
+        )
+
+    solve(work_ref, [lambda: couple(0), lambda: couple(half)])
+    target = chosen_sums(mean, work_ref[:, width:], 1, 1)
+    coupling = full_ref[...]
     coupling = coupling / samples - total.astype(jnp.float32)
     view = view_ref[...].astype(jnp.float32)
     grad = view - target + coupling

time: 114 us -> 112 us (0.982)
  Pallas kernels: 31.3 us -> 29.8 us
where the time goes in v7:
time: 112 us; the launch traced here: 111 us
  blocking collectives  63.1 us (56%)
  Pallas kernels  29.8 us (27%)
  waiting for transfers between devices  10.3 us (9%)
  starting transfers between devices  3.5 us (3%)
  local copies, waits for them, and re-layouts  2.34 us (2%)
    all_to_all x3, blocking collectives, swap(): return lax.all_to_all(x, axis, 0, 0, tiled=True, axis_index_groups=groups)  63.1 us
    pallas_call x1, Pallas kernels, encode(): pl.pallas_call(conv_kernel, out_shape=jax.ShapeDtypeStruct((got.shape[0],...  14.3 us
    pallas_call x1, Pallas kernels, finish(): pl.pallas_call(tail_kernel, out_shape=(jax.ShapeDtypeStruct((share, width...  12.5 us
    all_to_all x1, waiting for transfers between devices, swap(): return lax.all_to_all(x, axis, 0, 0, tiled=True, axis_index_groups=groups)  7.07 us
    all_to_all x1, starting transfers between devices, swap(): return lax.all_to_all(x, axis, 0, 0, tiled=True, axis_index_groups=groups)  3.41 us
  transfers between devices with their start and end apart: 3, of which 3 were waited for; matrix products, arithmetic and copies ran while one was open for 0% of the time, Pallas kernels for 0%

profile of v7, /device:TPU:0, one launch (start us, length us, event | category | flops | bytes accessed | tf_op | source)
XLA Modules:
  0.0 110.7 jit_solution(14922567294364124328)
XLA Ops:
  0.6 0.7 convert_element_type.14
  1.4 0.1 convert_element_type.15
  1.5 0.1 convert_element_type.17
  1.6 2.1 %copy.10 = bf16[8,64,8,256]{3,1,2,0:T(8,128)(2,1)S(1)} copy(bf16[8,64,8,256]{3,2,1,0:T(8,128)(2,1)} %bitcast.26) | data formatting | bytes 4194304 | tf_op jit(solution)/shard_map/reshape;squeeze | solution.py:425
  3.7 0.1 fusion.1
  3.8 0.0 copy-start
  3.8 0.0 copy-start.3
  3.9 34.2 %all_to_all.20.got_ref = bf16[8,520,256]{2,1,0:T(8,128)(2,1)S(1)} all-to-all(bf16[8,520,256]{2,1,0:T(8,128)(2,1)S(1)} %fusion.1), channel_id=1, replica_groups=mesh['mod'=16,'sp'=8] {'sp'}, dimensions={0} | all-to-all | bytes 4259840 | tf_op jit(solution)/shard_map/all_to_all | solution.py:415
  38.0 0.0 copy-done
  38.0 0.0 copy-done.3
  38.0 0.0 copy-start.1
  38.0 0.0 copy-start.2
  38.0 0.0 copy-start.4
  38.0 14.3 %encode.1 = bf16[8,64,256]{2,1,0:T(8,128)(2,1)} custom-call(bf16[8,520,256]{2,1,0:T(8,128)(2,1)S(1)} %all_to_all.20.got_ref, bf16[256,256]{1,0:T(8,128)(2,1)S(1)} %bitcast.23, bf16[4096,256]{1,0:T(8,128)(2,1)S(1)} %bitcast.19), custom_call_target="tpu_custom_call" | custom-call | tf_op jit(solution)/shard_map/encode/pallas_call | solution.py:117
  52.3 3.4 %all-to-all-start.1 = ((bf16[8,64,256]{2,1,0:T(8,128)(2,1)}), bf16[8,64,256]{2,1,0:T(8,128)(2,1)S(1)}, u32[]{:S(2)}, u32[]{:S(2)}) async-start(bf16[8,64,256]{2,1,0:T(8,128)(2,1)} %encode.1), calls=%async_computation.1 | async-start | bytes 524288 | tf_op jit(solution)/shard_map/all_to_all | solution.py:415
  55.8 0.1 pad_add_fusion.place_ref
  55.9 7.1 %all-to-all-done.1 = bf16[8,64,256]{2,1,0:T(8,128)(2,1)S(1)} async-done(((bf16[8,64,256]{2,1,0:T(8,128)(2,1)}), bf16[8,64,256]{2,1,0:T(8,128)(2,1)S(1)}, u32[]{:S(2)}, u32[]{:S(2)}) %all-to-all-start.1) | async-done | bytes 262176 | tf_op jit(solution)/shard_map/all_to_all | solution.py:415
  62.9 0.0 copy-done.1
  62.9 0.0 copy-done.2
  62.9 0.0 copy-done.4
  62.9 2.1 %view.1 = (bf16[64,512]{1,0:T(8,128)(2,1)S(1)}, bf16[512,256]{1,0:T(8,128)(2,1)S(1)}, f32[512,128]{1,0:T(8,128)S(1)}) custom-call(s32[2]{0:T(128)S(1)} %pad_add_fusion.place_ref, bf16[512,256]{1,0:T(8,128)(2,1)S(1)} %bitcast.20, bf16[256,512]{1,0:T(8,128)(2,1)S(1)} %bitcast.21, bf16[512,256]{1,0:T(8,128)(2,1)S(1)} %bitcast.22, s32[1,512]{1,0:T(1,128)S(1)} %bitcast.24), custom_call_target="tpu_custom_call" | custom-call | tf_op jit(solution)/shard_map/view/pallas_call | solution.py:174
  65.0 0.1 collective-permute-start
  65.1 1.5 %collective-permute-done.other_ref = bf16[512,256]{1,0:T(8,128)(2,1)S(1)} collective-permute-done((bf16[512,256]{1,0:T(8,128)(2,1)S(1)}, bf16[512,256]{1,0:T(8,128)(2,1)S(1)}, u32[]{:S(2)}, u32[]{:S(2)}) %collective-permute-start) | collective-permute-done | bytes 262176 | tf_op jit(solution)/shard_map/ppermute | solution.py:440
  66.7 0.9 pair.1
  67.5 16.7 %all_to_all.21.in_ref = bf16[8,96,256]{2,1,0:T(8,128)(2,1)S(1)} all-to-all(bf16[8,96,256]{2,1,0:T(8,128)(2,1)S(1)} %pair.1), channel_id=1, replica_groups={{0,16,32,48,64,80,96,112},{8,24,40,56,72,88,104,120},{1,17,33,49,65,81,..., dimensions={0} | all-to-all | bytes 786432 | tf_op jit(solution)/shard_map/all_to_all | solution.py:415
  84.3 0.1 sums.1
  84.3 12.2 %all_to_all.22.sums_ref = bf16[8,96,256]{2,1,0:T(8,128)(2,1)S(1)} all-to-all(bf16[8,96,256]{2,1,0:T(8,128)(2,1)S(1)} %sums.1), channel_id=1, replica_groups={{0,16,32,48,64,80,96,112},{8,24,40,56,72,88,104,120},{1,17,33,49,65,81,..., dimensions={0} | all-to-all | bytes 786432 | tf_op jit(solution)/shard_map/all_to_all | solution.py:415
  96.5 0.0 collective-permute-start.1
  96.5 1.7 %collective-permute-done.1.other_ref = bf16[8,96,256]{2,1,0:T(8,128)(2,1)S(1)} collective-permute-done((bf16[8,96,256]{2,1,0:T(8,128)(2,1)S(1)}, bf16[8,96,256]{2,1,0:T(8,128)(2,1)S(1)}, u32[]{:S(2)}, u32[]{:S(2)}) %collective-permute-start.1) | collective-permute-done | bytes 393248 | tf_op jit(solution)/shard_map/ppermute | solution.py:443
  98.2 12.5 %finish.1 = (f32[64,256]{1,0:T(8,128)}, bf16[64,256]{1,0:T(8,128)(2,1)}, f32[64,256]{1,0:T(8,128)}) custom-call(s32[2]{0:T(128)S(1)} %pad_add_fusion.place_ref, bf16[8,96,256]{2,1,0:T(8,128)(2,1)S(1)} %all_to_all.22.sums_ref, bf16[8,96,256]{2,1,0:T(8,128)(2,1)S(1)} %collective-permute-done.1.other_ref, bf16[512,256]{1,0:T(8,128)(2,1)S(1)} %get-tuple-element.9.view_ref, ...), custom_call_target="tpu_custom_call" | custom-call | tf_op jit(solution)/shard_map/finish/pallas_call | solution.py:396
  (1 shorter events, 0.0 us)
Async XLA Ops:
  3.8 34.2 %copy-start = (bf16[1,4096,256]{2,1,0:T(8,128)(2,1)S(1)}, bf16[1,4096,256]{2,1,0:T(8,128)(2,1)}, u32[]{:S(2)}) copy-start(bf16[1,4096,256]{2,1,0:T(8,128)(2,1)} %param.9) | copy-start | bytes 6291460
  3.8 34.2 %copy-start.3 = (bf16[1,256,256]{2,1,0:T(8,128)(2,1)S(1)}, bf16[1,256,256]{2,1,0:T(8,128)(2,1)}, u32[]{:S(2)}) copy-start(bf16[1,256,256]{2,1,0:T(8,128)(2,1)} %param.8) | copy-start | bytes 393220
  38.0 24.9 %copy-start.1 = (bf16[1,256,512]{2,1,0:T(8,128)(2,1)S(1)}, bf16[1,256,512]{2,1,0:T(8,128)(2,1)}, u32[]{:S(2)}) copy-start(bf16[1,256,512]{2,1,0:T(8,128)(2,1)} %param.10) | copy-start | bytes 786436
  38.0 24.9 %copy-start.2 = (bf16[1,512,256]{2,1,0:T(8,128)(2,1)S(1)}, bf16[1,512,256]{2,1,0:T(8,128)(2,1)}, u32[]{:S(2)}) copy-start(bf16[1,512,256]{2,1,0:T(8,128)(2,1)} %param.11) | copy-start | bytes 786436
  38.0 24.9 %copy-start.4 = (s32[512]{0:T(512)S(1)}, s32[512]{0:T(512)}, u32[]{:S(2)}) copy-start(s32[512]{0:T(512)} %param.13) | copy-start | bytes 6148
  52.3 10.6 %all-to-all-start.1 = ((bf16[8,64,256]{2,1,0:T(8,128)(2,1)}), bf16[8,64,256]{2,1,0:T(8,128)(2,1)S(1)}, u32[]{:S(2)}, u32[]{:S(2)}) async-start(bf16[8,64,256]{2,1,0:T(8,128)(2,1)} %encode.1), calls=%async_computation.1 | async-start | bytes 524288 | tf_op jit(solution)/shard_map/all_to_all | solution.py:415
  65.0 1.6 %collective-permute-start = (bf16[512,256]{1,0:T(8,128)(2,1)S(1)}, bf16[512,256]{1,0:T(8,128)(2,1)S(1)}, u32[]{:S(2)}, u32[]{:S(2)}) collective-permute-start(bf16[512,256]{1,0:T(8,128)(2,1)S(1)} %get-tuple-element.9.view_ref), channel_id=1, source_target_pairs={{0,8},{8,0},{16,24},{24,16},{32,40},{40,32},{48,56},{56,48},{64,72... | collective-permute-start | bytes 786440 | tf_op jit(solution)/shard_map/ppermute | solution.py:440
  96.5 1.7 %collective-permute-start.1 = (bf16[8,96,256]{2,1,0:T(8,128)(2,1)S(1)}, bf16[8,96,256]{2,1,0:T(8,128)(2,1)S(1)}, u32[]{:S(2)}, u32[]{:S(2)}) collective-permute-start(bf16[8,96,256]{2,1,0:T(8,128)(2,1)S(1)} %all_to_all.22.sums_ref), channel_id=1, source_target_pairs={{0,8},{8,0},{16,24},{24,16},{32,40},{40,32},{48,56},{56,48},{64,72... | collective-permute-start | bytes 1179656 | tf_op jit(solution)/shard_map/ppermute | solution.py:443

commit v8 on v7

--- a/solution.py
+++ b/solution.py
@@ -423,7 +423,8 @@
     share = samples // size
     rows = images.shape[2]
     x = images[0].reshape(size, share, rows, -1).transpose(0, 2, 1, 3)
-    valid = valid_mask[0].reshape(size, share, 2, 4).transpose(0, 3, 2, 1)
+    x, valid = lax.optimization_barrier((x, valid_mask))
+    valid = valid[0].reshape(size, share, 2, 4).transpose(0, 3, 2, 1)
     valid = valid.reshape(size, 4, 2 * share).astype(jnp.bfloat16)
     valid = jnp.pad(valid, ((0, 0), (0, EXTRA - 4), (0, 256 - 2 * share)))
     sent = jnp.concatenate([x.reshape(size, rows * share, -1), valid], axis=1)

time: 112 us -> 111 us (level)
  no operation moved by 1% of the time
where the time goes in v8:
time: 111 us; the launch traced here: 110 us
  blocking collectives  63.1 us (57%)
  Pallas kernels  29.8 us (27%)
  waiting for transfers between devices  10.3 us (9%)
  starting transfers between devices  3.5 us (3%)
  local copies, waits for them, and re-layouts  2.35 us (2%)
    all_to_all x3, blocking collectives, swap(): return lax.all_to_all(x, axis, 0, 0, tiled=True, axis_index_groups=groups)  63.1 us
    pallas_call x1, Pallas kernels, encode(): pl.pallas_call(conv_kernel, out_shape=jax.ShapeDtypeStruct((got.shape[0],...  14.3 us
    pallas_call x1, Pallas kernels, finish(): pl.pallas_call(tail_kernel, out_shape=(jax.ShapeDtypeStruct((share, width...  12.5 us
    all_to_all x1, waiting for transfers between devices, swap(): return lax.all_to_all(x, axis, 0, 0, tiled=True, axis_index_groups=groups)  7.07 us
    all_to_all x1, starting transfers between devices, swap(): return lax.all_to_all(x, axis, 0, 0, tiled=True, axis_index_groups=groups)  3.41 us
  transfers between devices with their start and end apart: 3, of which 3 were waited for; matrix products, arithmetic and copies ran while one was open for 0% of the time, Pallas kernels for 0%

profile of v8, /device:TPU:0, one launch (start us, length us, event | category | flops | bytes accessed | tf_op | source)
XLA Modules:
  0.0 110.0 jit_solution(13812089661886504650)
XLA Ops:
  0.6 0.0 copy-start.5
  0.6 2.1 %copy.14 = bf16[8,64,8,256]{3,1,2,0:T(8,128)(2,1)S(1)} copy(bf16[8,64,8,256]{3,2,1,0:T(8,128)(2,1)} %bitcast.27) | data formatting | bytes 4194304 | tf_op jit(solution)/shard_map/reshape;squeeze | solution.py:425
  2.8 0.0 copy-done.5
  2.8 0.1 convert_element_type.15
  2.9 0.1 convert_element_type.17
  3.0 0.1 fusion.1
  3.1 0.0 copy-start
  3.2 0.0 copy-start.3
  3.2 34.2 %all_to_all.20.got_ref = bf16[8,520,256]{2,1,0:T(8,128)(2,1)S(1)} all-to-all(bf16[8,520,256]{2,1,0:T(8,128)(2,1)S(1)} %fusion.1), channel_id=1, replica_groups=mesh['mod'=16,'sp'=8] {'sp'}, dimensions={0} | all-to-all | bytes 4259840 | tf_op jit(solution)/shard_map/all_to_all | solution.py:415
  37.3 0.0 copy-done
  37.3 0.0 copy-done.3
  37.3 0.0 copy-start.1
  37.3 0.0 copy-start.2
  37.4 0.0 copy-start.4
  37.4 14.3 %encode.1 = bf16[8,64,256]{2,1,0:T(8,128)(2,1)} custom-call(bf16[8,520,256]{2,1,0:T(8,128)(2,1)S(1)} %all_to_all.20.got_ref, bf16[256,256]{1,0:T(8,128)(2,1)S(1)} %bitcast.24, bf16[4096,256]{1,0:T(8,128)(2,1)S(1)} %bitcast.20), custom_call_target="tpu_custom_call" | custom-call | tf_op jit(solution)/shard_map/encode/pallas_call | solution.py:117
  51.7 3.4 %all-to-all-start.1 = ((bf16[8,64,256]{2,1,0:T(8,128)(2,1)}), bf16[8,64,256]{2,1,0:T(8,128)(2,1)S(1)}, u32[]{:S(2)}, u32[]{:S(2)}) async-start(bf16[8,64,256]{2,1,0:T(8,128)(2,1)} %encode.1), calls=%async_computation.1 | async-start | bytes 524288 | tf_op jit(solution)/shard_map/all_to_all | solution.py:415
  55.1 0.1 pad_add_fusion.place_ref
  55.2 7.1 %all-to-all-done.1 = bf16[8,64,256]{2,1,0:T(8,128)(2,1)S(1)} async-done(((bf16[8,64,256]{2,1,0:T(8,128)(2,1)}), bf16[8,64,256]{2,1,0:T(8,128)(2,1)S(1)}, u32[]{:S(2)}, u32[]{:S(2)}) %all-to-all-start.1) | async-done | bytes 262176 | tf_op jit(solution)/shard_map/all_to_all | solution.py:415
  62.2 0.0 copy-done.1
  62.2 0.0 copy-done.2
  62.2 0.0 copy-done.4
  62.2 2.1 %view.1 = (bf16[64,512]{1,0:T(8,128)(2,1)S(1)}, bf16[512,256]{1,0:T(8,128)(2,1)S(1)}, f32[512,128]{1,0:T(8,128)S(1)}) custom-call(s32[2]{0:T(128)S(1)} %pad_add_fusion.place_ref, bf16[512,256]{1,0:T(8,128)(2,1)S(1)} %bitcast.21, bf16[256,512]{1,0:T(8,128)(2,1)S(1)} %bitcast.22, bf16[512,256]{1,0:T(8,128)(2,1)S(1)} %bitcast.23, s32[1,512]{1,0:T(1,128)S(1)} %bitcast.25), custom_call_target="tpu_custom_call" | custom-call | tf_op jit(solution)/shard_map/view/pallas_call | solution.py:174
  64.4 0.1 collective-permute-start
  64.4 1.5 %collective-permute-done.other_ref = bf16[512,256]{1,0:T(8,128)(2,1)S(1)} collective-permute-done((bf16[512,256]{1,0:T(8,128)(2,1)S(1)}, bf16[512,256]{1,0:T(8,128)(2,1)S(1)}, u32[]{:S(2)}, u32[]{:S(2)}) %collective-permute-start) | collective-permute-done | bytes 262176 | tf_op jit(solution)/shard_map/ppermute | solution.py:441
  66.0 0.9 pair.1
  66.9 16.7 %all_to_all.21.in_ref = bf16[8,96,256]{2,1,0:T(8,128)(2,1)S(1)} all-to-all(bf16[8,96,256]{2,1,0:T(8,128)(2,1)S(1)} %pair.1), channel_id=1, replica_groups={{0,16,32,48,64,80,96,112},{8,24,40,56,72,88,104,120},{1,17,33,49,65,81,..., dimensions={0} | all-to-all | bytes 786432 | tf_op jit(solution)/shard_map/all_to_all | solution.py:415
  83.6 0.1 sums.1
  83.7 12.2 %all_to_all.22.sums_ref = bf16[8,96,256]{2,1,0:T(8,128)(2,1)S(1)} all-to-all(bf16[8,96,256]{2,1,0:T(8,128)(2,1)S(1)} %sums.1), channel_id=1, replica_groups={{0,16,32,48,64,80,96,112},{8,24,40,56,72,88,104,120},{1,17,33,49,65,81,..., dimensions={0} | all-to-all | bytes 786432 | tf_op jit(solution)/shard_map/all_to_all | solution.py:415
  95.8 0.0 collective-permute-start.1
  95.8 1.7 %collective-permute-done.1.other_ref = bf16[8,96,256]{2,1,0:T(8,128)(2,1)S(1)} collective-permute-done((bf16[8,96,256]{2,1,0:T(8,128)(2,1)S(1)}, bf16[8,96,256]{2,1,0:T(8,128)(2,1)S(1)}, u32[]{:S(2)}, u32[]{:S(2)}) %collective-permute-start.1) | collective-permute-done | bytes 393248 | tf_op jit(solution)/shard_map/ppermute | solution.py:444
  97.6 12.5 %finish.1 = (f32[64,256]{1,0:T(8,128)}, bf16[64,256]{1,0:T(8,128)(2,1)}, f32[64,256]{1,0:T(8,128)}) custom-call(s32[2]{0:T(128)S(1)} %pad_add_fusion.place_ref, bf16[8,96,256]{2,1,0:T(8,128)(2,1)S(1)} %all_to_all.22.sums_ref, bf16[8,96,256]{2,1,0:T(8,128)(2,1)S(1)} %collective-permute-done.1.other_ref, bf16[512,256]{1,0:T(8,128)(2,1)S(1)} %get-tuple-element.13.view_ref, ...), custom_call_target="tpu_custom_call" | custom-call | tf_op jit(solution)/shard_map/finish/pallas_call | solution.py:396
  (2 shorter events, 0.0 us)
Async XLA Ops:
  0.6 2.2 %copy-start.5 = (s32[1,512,2,4]{1,3,2,0:T(4,128)S(1)}, s32[1,512,2,4]{1,3,2,0:T(4,128)}, u32[]{:S(2)}) copy-start(s32[1,512,2,4]{1,3,2,0:T(4,128)} %param.12) | copy-start | bytes 49156
  3.1 34.2 %copy-start = (bf16[1,4096,256]{2,1,0:T(8,128)(2,1)S(1)}, bf16[1,4096,256]{2,1,0:T(8,128)(2,1)}, u32[]{:S(2)}) copy-start(bf16[1,4096,256]{2,1,0:T(8,128)(2,1)} %param.9) | copy-start | bytes 6291460
  3.2 34.2 %copy-start.3 = (bf16[1,256,256]{2,1,0:T(8,128)(2,1)S(1)}, bf16[1,256,256]{2,1,0:T(8,128)(2,1)}, u32[]{:S(2)}) copy-start(bf16[1,256,256]{2,1,0:T(8,128)(2,1)} %param.8) | copy-start | bytes 393220
  37.3 24.9 %copy-start.1 = (bf16[1,256,512]{2,1,0:T(8,128)(2,1)S(1)}, bf16[1,256,512]{2,1,0:T(8,128)(2,1)}, u32[]{:S(2)}) copy-start(bf16[1,256,512]{2,1,0:T(8,128)(2,1)} %param.10) | copy-start | bytes 786436
  37.3 24.9 %copy-start.2 = (bf16[1,512,256]{2,1,0:T(8,128)(2,1)S(1)}, bf16[1,512,256]{2,1,0:T(8,128)(2,1)}, u32[]{:S(2)}) copy-start(bf16[1,512,256]{2,1,0:T(8,128)(2,1)} %param.11) | copy-start | bytes 786436
  37.4 24.9 %copy-start.4 = (s32[512]{0:T(512)S(1)}, s32[512]{0:T(512)}, u32[]{:S(2)}) copy-start(s32[512]{0:T(512)} %param.13) | copy-start | bytes 6148
  51.7 10.6 %all-to-all-start.1 = ((bf16[8,64,256]{2,1,0:T(8,128)(2,1)}), bf16[8,64,256]{2,1,0:T(8,128)(2,1)S(1)}, u32[]{:S(2)}, u32[]{:S(2)}) async-start(bf16[8,64,256]{2,1,0:T(8,128)(2,1)} %encode.1), calls=%async_computation.1 | async-start | bytes 524288 | tf_op jit(solution)/shard_map/all_to_all | solution.py:415
  64.4 1.6 %collective-permute-start = (bf16[512,256]{1,0:T(8,128)(2,1)S(1)}, bf16[512,256]{1,0:T(8,128)(2,1)S(1)}, u32[]{:S(2)}, u32[]{:S(2)}) collective-permute-start(bf16[512,256]{1,0:T(8,128)(2,1)S(1)} %get-tuple-element.13.view_ref), channel_id=1, source_target_pairs={{0,8},{8,0},{16,24},{24,16},{32,40},{40,32},{48,56},{56,48},{64,72... | collective-permute-start | bytes 786440 | tf_op jit(solution)/shard_map/ppermute | solution.py:441
  95.8 1.7 %collective-permute-start.1 = (bf16[8,96,256]{2,1,0:T(8,128)(2,1)S(1)}, bf16[8,96,256]{2,1,0:T(8,128)(2,1)S(1)}, u32[]{:S(2)}, u32[]{:S(2)}) collective-permute-start(bf16[8,96,256]{2,1,0:T(8,128)(2,1)S(1)} %all_to_all.22.sums_ref), channel_id=1, source_target_pairs={{0,8},{8,0},{16,24},{24,16},{32,40},{40,32},{48,56},{56,48},{64,72... | collective-permute-start | bytes 1179656 | tf_op jit(solution)/shard_map/ppermute | solution.py:444
